TPU v7x, 32 devices: a whole 2x2x4 slice. The times are simulated.
32 devices in a mesh: groups: 2 (over y), row: 4 (over z), col: 2 (over x), chan: 2 (over core).
Axes of the slice: x: 2, y: 2, z: 4, core: 2. Of those that a mesh axis runs over, the one named last changes fastest.
Arguments:
- pair_input: bfloat16 [512, 256, 128], P(('groups', 'row'), ('col', 'chan')), parts along dimension 0, may hold values from -6 to 6
- alignment_features: bfloat16 [128, 512, 64], P('row', ('groups', 'col', 'chan')), parts along dimension 1, may hold values from -6 to 6
- alignment_mask: int32 [128, 512], P('row', ('groups', 'col', 'chan')), parts along dimension 1, may hold values from 0 to 1
- token_valid: int32 [512], P('groups'), parts along dimension 0, may hold values from 0 to 1, as said below
- left_weight: bfloat16 [64, 32], replicated, may hold values from -0.75 to 0.75
- right_weight: bfloat16 [64, 32], replicated, may hold values from -0.75 to 0.75
- output_weight: bfloat16 [1024, 128], replicated, may hold values from -1.75 to 1.75
- gate_weight: bfloat16 [128, 512], replicated, may hold values from -0.5 to 0.5
- up_weight: bfloat16 [128, 512], replicated, may hold values from -0.5 to 0.5
- down_weight: bfloat16 [512, 128], replicated, may hold values from -0.25 to 0.25
- kernel_weight: bfloat16 [3, 3, 128, 128], replicated, may hold values from -0.1875 to 0.1875
Outputs:
- pair_out: bfloat16 [512, 256, 128], P(('groups', 'row'), ('col', 'chan')), parts along dimension 0
There are 2 independent parts, one for each index of `groups`. A program takes and returns all parts, laid end to end along the dimension named above; an argument that names none is the same for every part. Nothing has to cross between parts.
Inputs may be any that keep to these rules, and one draw needn't show every extreme that they name: `token_valid`: the ones come first.
All inputs are finite; a program needn't handle non-finite values.
Results may differ from a plain program's by a relative error of at most 0.014.
Values may be sent and summed in bfloat16 or wider, within the bound.
A program may use at most 64 MiB of HBM per device.

v0:
```python
import functools

import jax
import jax.numpy as jnp
from jax import lax
from jax.experimental import pallas as pl
from jax.experimental.pallas import tpu as pltpu
from jax.sharding import PartitionSpec as P

epsilon = 1e-05
F32, BF16 = jnp.float32, jnp.bfloat16
MESH = pl.DeviceIdType.MESH
AROUND = [(a, b) for a in (-1, 0, 1) for b in (-1, 0, 1) if (a, b) != (0, 0)]


def dot(a, b):
    return jnp.dot(a, b, preferred_element_type=F32)


def block_kernel(
    sizes,
    feat_ref,
    mask_ref,
    valid_ref,
    wl_ref,
    wr_ref,
    *rest,
):
    far, (out_ref, *rest) = rest[:6], rest[6:]
    near, (w_sem, *rest) = rest[:6], rest[6:]
    pair_ref, wo_ref, wg_ref, wu_ref, wd_ref, wk_ref = near
    (
    proj,
    vrows,
    lsend,
    lg,
    rg,
    rt,
    rq,
    lcat,
    wof,
    w4,
    zs,
    rexp,
    ones,
    two,
    mirror,
    mf,
    sym,
    wide,
    colf,
    hsend,
    hrecv,
    l1_send,
    l1_recv,
    l2_send,
    l2_recv,
    r_send,
    r_recv,
    m_send,
    m_recv,
    relay,
    rl_send,
    rl_recv,
    h_send,
    h_recv,
    ) = rest
    rn, cn, chans, fold, rd, cd, ch, sl, tl, pw, cr = sizes
    row = lax.axis_index("row")
    col = lax.axis_index("col") * chans + lax.axis_index("chan")
    per = 128 // pw
    lgroups, rgroups = rd // per, cd // per
    depth = rn * sl
    steps = rd // cr
    cgroups = cr // per

    def at(r, c):
        return {"row": r, "col": c // chans, "chan": c % chans}

    def remote(src, dst, ssem, rsem, r, c):
        return pltpu.make_async_remote_copy(
            src_ref=src, dst_ref=dst, send_sem=ssem, recv_sem=rsem,
            device_id=at(r, c), device_id_type=MESH,
        )

    order = (1, 0, 2, 3, 4, 5)
    loads = [pltpu.make_async_copy(far[n], near[n], w_sem.at[n]) for n in range(6)]
    for n in order:
        loads[n].start()
    hrecv[...] = jnp.zeros_like(hrecv)
    barrier = pltpu.get_barrier_semaphore()

    def greet(n, carry):
        pl.semaphore_signal(barrier, inc=1, device_id=at(n // cn, n % cn), device_id_type=MESH)
        return carry

    lax.fori_loop(0, rn * cn, greet, 0)

    spread = (
        lax.broadcasted_iota(jnp.int32, (pw, 128), 1) % pw
        == lax.broadcasted_iota(jnp.int32, (pw, 128), 0)
    ).astype(F32).astype(BF16)
    mask = mask_ref[...].astype(F32).astype(BF16)
    spots = tl // per
    token_of = (
        lax.broadcasted_iota(jnp.int32, (tl, spots * 128), 1) // pw
        == lax.broadcasted_iota(jnp.int32, (tl, spots * 128), 0)
    ).astype(F32).astype(BF16)
    wide_mask = dot(mask, token_of)
    feats = feat_ref[...].reshape(sl * tl, feat_ref.shape[2])
    lane_of = lax.broadcasted_iota(jnp.int32, (sl, 128), 1) // pw

    def project(n, w_ref):
        tiled = lax.dot_general(
            w_ref[...], spread, (((0,), (0,)), ((), ())), preferred_element_type=F32
        ).astype(BF16)
        proj[n] = dot(feats, tiled)
        parts = []
        for g in range(spots):
            got = proj[n, pl.ds(g * per, sl, stride=tl), :]
            for t in range(1, per):
                other = proj[n, pl.ds(g * per + t, sl, stride=tl), :]
                got = jnp.where(lane_of == t, other, got)
            parts.append((got * wide_mask[:, g * 128 : (g + 1) * 128]).astype(BF16))
        return parts

    left = project(0, wl_ref)
    right = project(1, wr_ref)
    for k in range(fold):
        for g in range(lgroups):
            lsend[k, 1 + g] = left[k * lgroups + g]
        lsend[k, 0] = jnp.zeros((sl, 128), BF16)
        lsend[k, 0, :, 0:rd] = mask[:, k * rd : (k + 1) * rd]
    for g in range(rgroups):
        rg[row, g] = right[g]
    rg[row, rgroups] = jnp.zeros((sl, 128), BF16)
    rg[row, rgroups, :, 0:tl] = mask

    pl.semaphore_wait(barrier, rn * cn)

    def span(n):
        if isinstance(n, int) and n == 0:
            return pl.ds(0, cgroups + 1)
        return pl.ds(1 + n * cgroups, cgroups)

    def l1_target(k):
        to_row, to_col = col * fold + k, row % cn
        return to_row, to_col, jnp.logical_and(to_row == row, to_col == col)

    def send_left(n):
        for k in range(fold):
            to_row, to_col, mine = l1_target(k)
            slot = row // cn
            src, dst = lsend.at[k, span(n)], lg.at[row, span(n)]

            @pl.when(mine)
            def _():
                pltpu.make_async_copy(src, dst, l1_recv.at[slot, n]).start()

            @pl.when(jnp.logical_not(mine))
            def _():
                remote(src, dst, l1_send.at[k, n], l1_recv.at[slot, n], to_row, to_col).start()

    def spread_left(n):
        for m in range(fold):
            piece = lg.at[col + m * cn, span(n)]
            pltpu.make_async_copy(piece, piece, l1_recv.at[m, n]).wait()
            for d in range(1, cn):
                remote(
                    piece, piece, l2_send.at[m, d - 1, n], l2_recv.at[m, d - 1, n],
                    row, (col + d) % cn,
                ).start()

    def take_left(n):
        for m in range(fold):
            for d in range(1, cn):
                piece = lg.at[(col + cn - d) % cn + m * cn, span(n)]
                pltpu.make_async_copy(piece, piece, l2_recv.at[m, d - 1, n]).wait()

    send_left(0)

    def chain(t):
        low, high = jnp.maximum(row - t, 0), jnp.minimum(row + t, rn - 1)
        ups = jnp.logical_and(row - t >= 0, row + 1 < rn)
        downs = jnp.logical_and(row + t < rn, row >= 1)
        return (ups, low, row + 1), (downs, high, row - 1)

    cut = rgroups // 2
    pieces = (pl.ds(0, cut), pl.ds(cut, rgroups + 1 - cut))

    def pass_on(t):
        for way, (go, slot, to_row) in enumerate(chain(t)):

            @pl.when(go)
            def _():
                for e, piece in enumerate(pieces):
                    part_of = rg.at[slot, piece]
                    remote(
                        part_of, part_of, r_send.at[way, t, e], r_recv.at[slot, e], to_row, col
                    ).start()

    pass_on(0)
    for n in range(1, steps):
        send_left(n)

    tokens = valid_ref.shape[1]
    valid = valid_ref[...].astype(F32)

    def as_rows(first, count):
        hit = lax.broadcasted_iota(jnp.int32, (count, tokens), 1) == first + (
            lax.broadcasted_iota(jnp.int32, (count, tokens), 0)
        )
        chosen = jnp.where(hit, jnp.broadcast_to(valid, (count, tokens)), 0.0).astype(BF16)
        return dot(chosen, jnp.ones((tokens, ch), BF16))

    vrows[0:rd] = as_rows(row * rd, rd)
    valid_cols = as_rows(col * cd, cd)

    loads[1].wait()
    wof[...] = wo_ref[...].astype(F32)
    w4[...] = jnp.zeros_like(w4)
    for q in range(pw):
        part = wof[pl.ds(q, pw, stride=pw), :].astype(BF16)
        for i in range(per):
            w4[q * 128 + i * pw : q * 128 + (i + 1) * pw, i * ch : (i + 1) * ch] = part

    spread_left(0)
    for t in range(rn - 1):
        for e, piece in enumerate(pieces):
            for way, (there_is, slot) in enumerate((
                (row - t - 1 >= 0, jnp.maximum(row - t - 1, 0)),
                (row + t + 1 < rn, jnp.minimum(row + t + 1, rn - 1)),
            )):

                @pl.when(there_is)
                def _():
                    part_of = rg.at[slot, piece]
                    pltpu.make_async_copy(part_of, part_of, r_recv.at[slot, e]).wait()

                if t + 1 < rn - 1:
                    go, _slot, to_row = chain(t + 1)[way]

                    @pl.when(go)
                    def _():
                        part_of = rg.at[slot, piece]
                        remote(
                            part_of, part_of, r_send.at[way, t + 1, e], r_recv.at[slot, e],
                            to_row, col,
                        ).start()

    for n in range(1, steps):
        spread_left(n)
    for g in range(rgroups):
        slab = rg[:, g].astype(F32).reshape(depth, 128)
        rt[g * 128 : (g + 1) * 128, :] = slab.T
    for q in range(pw):
        rq[q * cd : (q + 1) * cd, :] = rt[pl.ds(q, cd, stride=pw), :].astype(BF16)

    take_left(0)
    left_mask = lg[:, 0].astype(F32).reshape(depth, 128)
    right_mask = rg[:, rgroups].astype(F32).reshape(depth, 128)
    counts = dot(right_mask.T.astype(BF16), left_mask.astype(BF16))
    inverse = 1.0 / jnp.maximum(counts, 1.0)
    for i in range(rd):
        rexp[i] = jnp.broadcast_to(inverse[0:cd, i : i + 1], (cd, ch))

    for n in (0, 2, 3, 4, 5):
        loads[n].wait()

    qstep = min(8, pw)

    part = cr // 2

    def to_mirror(step, k, p):
        begin = step * cr + p * part
        src = two.at[pl.ds(begin, part), pl.ds(k * rd, rd)]
        dst = mirror.at[pl.ds((row % fold) * rd + begin, part)]
        return src, dst

    def send_mirror(step, k, p):
        to_row, to_col = col * fold + k, row // fold
        mine = jnp.logical_and(to_row == row, to_col == col)
        across = to_col // chans != col // chans
        src, dst = to_mirror(step, k, p)
        rsem = m_recv.at[row % fold, step, p]
        ssem = m_send.at[k, step, p]

        @pl.when(mine)
        def _():
            pltpu.make_async_copy(src, dst, rsem).start()

        direct = jnp.logical_not(mine)
        if p == 1:
            direct = jnp.logical_and(direct, jnp.logical_not(across))

            @pl.when(across)
            def _():
                slot, core = to_row // chans, to_row % chans
                remote(
                    src, relay.at[slot, step], ssem, rl_recv.at[slot, step], row,
                    to_col // chans * chans + core,
                ).start()

        @pl.when(direct)
        def _():
            remote(src, dst, ssem, rsem, to_row, to_col).start()

    def relayed(m):
        key = m * chans + col % chans
        from_col, to_row, to_col = key // fold, key, row // fold
        active = jnp.logical_and(
            to_col // chans == col // chans, from_col // chans != to_col // chans
        )
        return active, row, to_row, to_col

    def forward(step):
        for m in range(rn // chans):
            active, from_row, to_row, to_col = relayed(m)

            @pl.when(active)
            def _():
                piece = relay.at[m, step]
                pltpu.make_async_copy(piece, piece, rl_recv.at[m, step]).wait()
                begin = (from_row % fold) * rd + step * cr + part
                remote(
                    piece, mirror.at[pl.ds(begin, part)], rl_send.at[m, step],
                    m_recv.at[from_row % fold, step, 1], to_row, to_col,
                ).start()

    lag = min(1, steps)

    def one_step(step, carry):

        @pl.when(step > 0)
        def _():
            take_left(step)

        for g in range(cgroups):
            slab = lg[:, 1 + step * cgroups + g].astype(F32).reshape(depth, 128)
            lcat[0, :, g * 128 : (g + 1) * 128] = slab.astype(BF16)
        lpart = lcat[0]
        for q0 in range(0, pw, qstep):
            z = dot(rq[q0 * cd : (q0 + qstep) * cd, :], lpart).astype(BF16)
            for q in range(qstep):
                for g in range(cgroups):
                    zs[g * cd : (g + 1) * cd, (q0 + q) * 128 : (q0 + q + 1) * 128] = z[
                        q * cd : (q + 1) * cd, g * 128 : (g + 1) * 128
                    ]
        update = dot(zs[...], w4[...])
        for g in range(cgroups):
            for i in range(per):
                at_row = step * cr + g * per + i
                add = update[g * cd : (g + 1) * cd, i * ch : (i + 1) * ch] * rexp[at_row]
                ones[g * per + i] = (pair_ref[at_row].astype(F32) + add).astype(BF16)
        for p in (1, 0):
            values = ones[p * part : (p + 1) * part].reshape(part * cd, ch).astype(F32)
            centre = jnp.mean(values, axis=-1, keepdims=True)
            shifted = values - centre
            var = jnp.mean(jnp.square(shifted), axis=-1, keepdims=True)
            normed = (shifted * lax.rsqrt(var + epsilon)).astype(BF16)
            gate = dot(normed, wg_ref[...])
            up = dot(normed, wu_ref[...])
            hidden = (gate / (1.0 + jnp.exp(-gate)) * up).astype(BF16)
            result = (values + dot(hidden, wd_ref[...])).astype(BF16)
            two[pl.ds(step * cr + p * part, part)] = result.reshape(part, cd, ch)
            for k in range(fold):
                send_mirror(step, k, p)
            if p == 1:

                @pl.when(step >= lag)
                def _():
                    forward(step - lag)

        return carry

    lax.fori_loop(0, steps, one_step, 0)
    for step in range(steps - lag, steps):
        forward(step)

    for step in range(steps):
        for k in range(fold):
            begin = k * rd + step * cr
            for p in (0, 1):
                piece = mirror.at[pl.ds(begin + p * part, part)]
                pltpu.make_async_copy(piece, piece, m_recv.at[k, step, p]).wait()
            mf[begin * rd : (begin + cr) * rd, :] = (
                mirror[begin : begin + cr].astype(F32).reshape(cr * rd, ch)
            )
            some_cols = valid_cols[begin : begin + cr]

            def one_row(i, carry):
                other = mf[pl.ds(begin * rd + i, cr, stride=rd), :]
                half_sum = (two[i, begin : begin + cr].astype(F32) + other) * 0.5
                sym[i, begin : begin + cr] = half_sum
                masked = half_sum * some_cols * vrows[pl.ds(i, 1), :]
                wide[i + 1, begin : begin + cr, ch : 2 * ch] = masked.astype(BF16)
                if begin == 0:
                    colf[0, pl.ds(i, 1), :] = masked[0:1]
                if begin + cr == cd:
                    colf[1, pl.ds(i, 1), :] = masked[cr - 1 : cr]
                return carry

            lax.fori_loop(0, rd, one_row, 0, unroll=4)

    for n, (a, b) in enumerate(AROUND):
        if b == 0:
            hsend[n, 0:cd] = wide[1 if a < 0 else rd, :, ch : 2 * ch]
        elif a == 0:
            hsend[n, 0:rd] = colf[0 if b < 0 else 1].astype(BF16)
        else:
            corner = colf[0 if b < 0 else 1, 0:1] if a < 0 else colf[0 if b < 0 else 1, rd - 1 : rd]
            hsend[n, 0:16] = jnp.broadcast_to(corner, (16, ch)).astype(BF16)

    def there(a, b):
        r, c = row + a, col + b
        return jnp.logical_and(
            jnp.logical_and(r >= 0, r < rn), jnp.logical_and(c >= 0, c < cn)
        )

    def lines(a, b):
        return cd if b == 0 else (rd if a == 0 else 16)

    for n, (a, b) in enumerate(AROUND):

        @pl.when(there(a, b))
        def _():
            size = lines(a, b)
            remote(
                hsend.at[n, pl.ds(0, size)], hrecv.at[n, pl.ds(0, size)], h_send.at[n],
                h_recv.at[n], row + a, col + b,
            ).start()

    place = lax.broadcasted_iota(jnp.int32, (cd, ch), 0)

    def widen(i, before, after):
        centre = wide[i, :, ch : 2 * ch].astype(F32)
        wide[i, :, 0:ch] = jnp.where(place == 0, before, pltpu.roll(centre, 1, 0)).astype(BF16)
        wide[i, :, 2 * ch : 3 * ch] = jnp.where(
            place == cd - 1, after, pltpu.roll(centre, cd - 1, 0)
        ).astype(BF16)

    def widen_row(i, carry):
        widen(i + 1, 0.0, 0.0)
        return carry

    lax.fori_loop(0, rd, widen_row, 0, unroll=4)

    for n, (a, b) in enumerate(AROUND):

        @pl.when(there(-a, -b))
        def _():
            piece = hrecv.at[n, pl.ds(0, lines(a, b))]
            pltpu.make_async_copy(piece, piece, h_recv.at[n]).wait()

    slot_of = {direction: n for n, direction in enumerate(AROUND)}
    wide[0, :, ch : 2 * ch] = hrecv[slot_of[(1, 0)], 0:cd]
    wide[rd + 1, :, ch : 2 * ch] = hrecv[slot_of[(-1, 0)], 0:cd]
    colf[0] = hrecv[slot_of[(0, 1)], 0:rd].astype(F32)
    colf[1] = hrecv[slot_of[(0, -1)], 0:rd].astype(F32)
    edge = lax.broadcasted_iota(jnp.int32, (16, ch), 0)

    def patch_row(i, carry):
        first = wide[i + 1, 0:16, 0:ch].astype(F32)
        wide[i + 1, 0:16, 0:ch] = jnp.where(
            edge == 0, colf[0, pl.ds(i, 1), :], first
        ).astype(BF16)
        last = wide[i + 1, cd - 16 : cd, 2 * ch : 3 * ch].astype(F32)
        wide[i + 1, cd - 16 : cd, 2 * ch : 3 * ch] = jnp.where(
            edge == 15, colf[1, pl.ds(i, 1), :], last
        ).astype(BF16)
        return carry

    lax.fori_loop(0, rd, patch_row, 0, unroll=4)
    widen(
        0,
        hrecv[slot_of[(1, 1)], 0:16].astype(F32)[0:1],
        hrecv[slot_of[(1, -1)], 0:16].astype(F32)[0:1],
    )
    widen(
        rd + 1,
        hrecv[slot_of[(-1, 1)], 0:16].astype(F32)[0:1],
        hrecv[slot_of[(-1, -1)], 0:16].astype(F32)[0:1],
    )

    strip = 8

    def conv(n, carry):
        total = sym[pl.ds(n * strip, strip)].reshape(strip * cd, ch)
        for a in range(3):
            window = wide[pl.ds(n * strip + a, strip)].reshape(strip * cd, 3 * ch)
            total = total + dot(window, wk_ref[a])
        out_ref[pl.ds(n * strip, strip)] = total.astype(BF16).reshape(strip, cd, ch)
        return carry

    lax.fori_loop(0, rd // strip, conv, 0)

    for k in range(fold):
        @pl.when(jnp.logical_not(l1_target(k)[2]))
        def _():
            for n in range(steps):
                piece = lsend.at[k, span(n)]
                pltpu.make_async_copy(piece, piece, l1_send.at[k, n]).wait()

        to_row, to_col = col * fold + k, row // fold

        @pl.when(jnp.logical_not(jnp.logical_and(to_row == row, to_col == col)))
        def _():
            for step in range(steps):
                for p in (0, 1):
                    src, _dst = to_mirror(step, k, p)
                    pltpu.make_async_copy(src, src, m_send.at[k, step, p]).wait()

    for m in range(rn // chans):

        @pl.when(relayed(m)[0])
        def _():
            for step in range(steps):
                piece = relay.at[m, step]
                pltpu.make_async_copy(piece, piece, rl_send.at[m, step]).wait()

    for t in range(rn - 1):
        for way, (go, slot, _to_row) in enumerate(chain(t)):

            @pl.when(go)
            def _():
                for e, piece in enumerate(pieces):
                    part_of = rg.at[slot, piece]
                    pltpu.make_async_copy(part_of, part_of, r_send.at[way, t, e]).wait()

    for m in range(fold):
        for d in range(1, cn):
            for n in range(steps):
                piece = lg.at[col + m * cn, span(n)]
                pltpu.make_async_copy(piece, piece, l2_send.at[m, d - 1, n]).wait()
    for n, (a, b) in enumerate(AROUND):

        @pl.when(there(a, b))
        def _():
            piece = hsend.at[n, pl.ds(0, lines(a, b))]
            pltpu.make_async_copy(piece, piece, h_send.at[n]).wait()


def on_device(
    mesh_shape,
    pair_input,
    alignment_features,
    alignment_mask,
    token_valid,
    left_weight,
    right_weight,
    output_weight,
    gate_weight,
    up_weight,
    down_weight,
    kernel_weight,
):
    rd, cd, ch = pair_input.shape
    sl, tl, aw = alignment_features.shape
    pw = left_weight.shape[1]
    hid = gate_weight.shape[1]
    rn, chans = mesh_shape["row"], mesh_shape["chan"]
    cn = mesh_shape["col"] * chans
    fold = rn // cn
    per = 128 // pw
    cr = min(16, rd)
    depth = rn * sl
    steps = rd // cr
    tall = max(rd, cd, 16)
    wk = kernel_weight.reshape(3, 3 * ch, ch)
    sizes = (rn, cn, chans, fold, rd, cd, ch, sl, tl, pw, cr)
    large = (pair_input, output_weight, gate_weight, up_weight, down_weight, wk)
    dma = pltpu.SemaphoreType.DMA
    vmem = pl.BlockSpec(memory_space=pltpu.VMEM)
    return pl.pallas_call(
        functools.partial(block_kernel, sizes),
        out_shape=jax.ShapeDtypeStruct((rd, cd, ch), BF16),
        in_specs=[vmem] * 5 + [pl.BlockSpec(memory_space=pl.ANY)] * 6,
        out_specs=vmem,
        scratch_shapes=[
            *[pltpu.VMEM(value.shape, value.dtype) for value in large],
            dma((6,)),
            pltpu.VMEM((2, sl * tl, 128), F32),
            pltpu.VMEM((tall, ch), F32),
            pltpu.VMEM((fold, rd // per + 1, sl, 128), BF16),
            pltpu.VMEM((rn, rd // per + 1, sl, 128), BF16),
            pltpu.VMEM((rn, cd // per + 1, sl, 128), BF16),
            pltpu.VMEM((cd * pw, depth), F32),
            pltpu.VMEM((pw * cd, depth), BF16),
            pltpu.VMEM((1, depth, cr * pw), BF16),
            pltpu.VMEM((pw * pw, ch), F32),
            pltpu.VMEM((pw * 128, per * ch), BF16),
            pltpu.VMEM((cr // per * cd, pw * 128), BF16),
            pltpu.VMEM((rd, cd, ch), F32),
            pltpu.VMEM((cr, cd, ch), BF16),
            pltpu.VMEM((rd, cd, ch), BF16),
            pltpu.VMEM((cd, rd, ch), BF16),
            pltpu.VMEM((cd * rd, ch), F32),
            pltpu.VMEM((rd, cd, ch), F32),
            pltpu.VMEM((rd + 2, cd, 3 * ch), BF16),
            pltpu.VMEM((2, rd, ch), F32),
            pltpu.VMEM((8, tall, ch), BF16),
            pltpu.VMEM((8, tall, ch), BF16),
            dma((fold, steps)),
            dma((fold, steps)),
            dma((fold, cn - 1, steps)),
            dma((fold, cn - 1, steps)),
            dma((2, rn - 1, 2)),
            dma((rn, 2)),
            dma((fold, steps, 2)),
            dma((fold, steps, 2)),
            pltpu.VMEM((rn // chans, steps, cr // 2, rd, ch), BF16),
            dma((rn // chans, steps)),
            dma((rn // chans, steps)),
            dma((8,)),
            dma((8,)),
        ],
        compiler_params=pltpu.CompilerParams(
            collective_id=0, has_side_effects=True, vmem_limit_bytes=60 * 1024 * 1024
        ),
    )(
        alignment_features,
        alignment_mask,
        token_valid.reshape(1, -1),
        left_weight.T,
        right_weight.T,
        *large,
    )


def solution(mesh):
    placed = (
        P(("groups", "row"), ("col", "chan"), None),
        P("row", ("groups", "col", "chan"), None),
        P("row", ("groups", "col", "chan")),
        P("groups"),
        P(),
        P(),
        P(),
        P(),
        P(),
        P(),
        P(),
    )
    return jax.shard_map(
        functools.partial(on_device, dict(mesh.shape)),
        mesh=mesh,
        in_specs=placed,
        out_specs=P(("groups", "row"), ("col", "chan"), None),
        check_vma=False,
    )
```

profile of v0, /device:TPU:1, one launch (start us, length us, event | category | flops | bytes accessed | tf_op | source)
XLA Modules:
  0.0 63.6 jit_solution(1320436460327045423)
XLA Ops:
  0.0 61.4 %shard_map.109 = bf16[64,64,128]{2,1,0:T(8,128)(2,1)} custom-call(bf16[32,64,64]{2,1,0:T(8,128)(2,1)} %feat_ref.1, s32[32,64]{1,0:T(8,128)} %mask_ref.1, s32[1,256]{1,0:T(1,128)} %bitcast.7, bf16[32,64]{1,0:T(8,128)(2,1)} %bitcast.5, bf16[32,64]{1,0:T(8,128)(2,1)} %bitcast.6, bf16[64,64,128]{2,1,0:T(8,128)(2,1)} %rest_0_.1, bf16[1024,128]{1,0:T(8,128)(2,1)} %rest_1_.1, ...), custom_call_target="tpu_custom_call" | custom-call | tf_op jit(solution)/shard_map/pallas_call | solution.py:574
  61.4 2.3 %copy.13 = bf16[64,64,128]{2,1,0:T(8,128)(2,1)} copy(bf16[64,64,128]{2,1,0:T(8,128)(2,1)} %shard_map.109) | data formatting | bytes 2097152
where the time goes:
time: 64.1 us; the launch traced here: 63.6 us
  Pallas kernels  61.4 us (96%)
  local copies, waits for them, and re-layouts  2.26 us (4%)
    pallas_call x1, Pallas kernels, on_device(): pl.pallas_call(functools.partial(block_kernel, sizes), out_shape=jax.Shap...  61.4 us
    unnamed x1, local copies, waits for them, and re-layouts  2.26 us

commit v1 on v0

--- a/solution.py
+++ b/solution.py
@@ -53,6 +53,7 @@
     hrecv,
     l1_send,
     l1_recv,
+    x_send,
     l2_send,
     l2_recv,
     r_send,
@@ -70,6 +71,7 @@
     col = lax.axis_index("col") * chans + lax.axis_index("chan")
     per = 128 // pw
     lgroups, rgroups = rd // per, cd // per
+    cuts = min(4, rgroups)
     depth = rn * sl
     steps = rd // cr
     cgroups = cr // per
@@ -88,6 +90,8 @@
     for n in order:
         loads[n].start()
     hrecv[...] = jnp.zeros_like(hrecv)
+    for i in (0, rd + 1):
+        wide[i] = jnp.zeros((cd, 3 * ch), BF16)
     barrier = pltpu.get_barrier_semaphore()
 
     def greet(n, carry):
@@ -125,17 +129,11 @@
         return parts
 
     left = project(0, wl_ref)
-    right = project(1, wr_ref)
     for k in range(fold):
         for g in range(lgroups):
             lsend[k, 1 + g] = left[k * lgroups + g]
         lsend[k, 0] = jnp.zeros((sl, 128), BF16)
         lsend[k, 0, :, 0:rd] = mask[:, k * rd : (k + 1) * rd]
-    for g in range(rgroups):
-        rg[row, g] = right[g]
-    rg[row, rgroups] = jnp.zeros((sl, 128), BF16)
-    rg[row, rgroups, :, 0:tl] = mask
-
     pl.semaphore_wait(barrier, rn * cn)
 
     def span(n):
@@ -143,14 +141,19 @@
             return pl.ds(0, cgroups + 1)
         return pl.ds(1 + n * cgroups, cgroups)
 
+    core, chip = col % chans, col // chans
+    held = rn // chans
+    home = row // fold // chans
+    is_home = chip == home
+
     def l1_target(k):
-        to_row, to_col = col * fold + k, row % cn
+        to_row, to_col = col * fold + k, chip * chans + row % chans
         return to_row, to_col, jnp.logical_and(to_row == row, to_col == col)
 
     def send_left(n):
         for k in range(fold):
             to_row, to_col, mine = l1_target(k)
-            slot = row // cn
+            slot = row // chans
             src, dst = lsend.at[k, span(n)], lg.at[row, span(n)]
 
             @pl.when(mine)
@@ -161,23 +164,39 @@
             def _():
                 remote(src, dst, l1_send.at[k, n], l1_recv.at[slot, n], to_row, to_col).start()
 
-    def spread_left(n):
-        for m in range(fold):
-            piece = lg.at[col + m * cn, span(n)]
+    chips = cn // chans
+
+    def spread_left(i, at_home):
+        m = (row // chans + i) % held
+        for n in range(steps):
+            piece = lg.at[m * chans + core, span(n)]
             pltpu.make_async_copy(piece, piece, l1_recv.at[m, n]).wait()
-            for d in range(1, cn):
+            if at_home:
+                for d in range(1, chips):
+                    remote(
+                        piece, piece, x_send.at[m, d - 1, n], l1_recv.at[m, n],
+                        row, (chip + d) % chips * chans + core,
+                    ).start()
+            for e in range(1, chans):
                 remote(
-                    piece, piece, l2_send.at[m, d - 1, n], l2_recv.at[m, d - 1, n],
-                    row, (col + d) % cn,
+                    piece, piece, l2_send.at[m, e - 1, n], l2_recv.at[m, e - 1, n],
+                    row, chip * chans + (core + e) % chans,
                 ).start()
 
     def take_left(n):
-        for m in range(fold):
-            for d in range(1, cn):
-                piece = lg.at[(col + cn - d) % cn + m * cn, span(n)]
-                pltpu.make_async_copy(piece, piece, l2_recv.at[m, d - 1, n]).wait()
-
-    send_left(0)
+        for m in range(held):
+            for e in range(1, chans):
+                piece = lg.at[m * chans + (core + chans - e) % chans, span(n)]
+                pltpu.make_async_copy(piece, piece, l2_recv.at[m, e - 1, n]).wait()
+
+    for n in range(steps):
+        send_left(n)
+
+    right = project(1, wr_ref)
+    for g in range(rgroups):
+        rg[row, 1 + g] = right[g]
+    rg[row, 0] = jnp.zeros((sl, 128), BF16)
+    rg[row, 0, :, 0:tl] = mask
 
     def chain(t):
         low, high = jnp.maximum(row - t, 0), jnp.minimum(row + t, rn - 1)
@@ -185,23 +204,26 @@
         downs = jnp.logical_and(row + t < rn, row >= 1)
         return (ups, low, row + 1), (downs, high, row - 1)
 
-    cut = rgroups // 2
-    pieces = (pl.ds(0, cut), pl.ds(cut, rgroups + 1 - cut))
-
-    def pass_on(t):
-        for way, (go, slot, to_row) in enumerate(chain(t)):
-
-            @pl.when(go)
+    quarter = rgroups // cuts
+    pieces = [
+        pl.ds(1 + e * quarter, quarter) if e else pl.ds(0, 1 + quarter) for e in range(cuts)
+    ]
+
+    upward = chip < chips // 2
+
+    def pass_on(urgent):
+        for way, (go, slot, to_row) in enumerate(chain(0)):
+
+            @pl.when(jnp.logical_and(go, upward == (urgent == (way == 0))))
             def _():
                 for e, piece in enumerate(pieces):
                     part_of = rg.at[slot, piece]
                     remote(
-                        part_of, part_of, r_send.at[way, t, e], r_recv.at[slot, e], to_row, col
+                        part_of, part_of, r_send.at[way, 0, e], r_recv.at[slot, e], to_row, col
                     ).start()
 
-    pass_on(0)
-    for n in range(1, steps):
-        send_left(n)
+    pass_on(True)
+    pass_on(False)
 
     tokens = valid_ref.shape[1]
     valid = valid_ref[...].astype(F32)
@@ -224,41 +246,82 @@
         for i in range(per):
             w4[q * 128 + i * pw : q * 128 + (i + 1) * pw, i * ch : (i + 1) * ch] = part
 
-    spread_left(0)
-    for t in range(rn - 1):
+    def hop(t, way):
+        there_is, slot = (
+            (row - t - 1 >= 0, jnp.maximum(row - t - 1, 0)),
+            (row + t + 1 < rn, jnp.minimum(row + t + 1, rn - 1)),
+        )[way]
         for e, piece in enumerate(pieces):
-            for way, (there_is, slot) in enumerate((
-                (row - t - 1 >= 0, jnp.maximum(row - t - 1, 0)),
-                (row + t + 1 < rn, jnp.minimum(row + t + 1, rn - 1)),
-            )):
-
-                @pl.when(there_is)
+
+            @pl.when(there_is)
+            def _():
+                part_of = rg.at[slot, piece]
+                pltpu.make_async_copy(part_of, part_of, r_recv.at[slot, e]).wait()
+
+            if t + 1 < rn - 1:
+                go, _slot, to_row = chain(t + 1)[way]
+
+                @pl.when(go)
                 def _():
                     part_of = rg.at[slot, piece]
-                    pltpu.make_async_copy(part_of, part_of, r_recv.at[slot, e]).wait()
-
-                if t + 1 < rn - 1:
-                    go, _slot, to_row = chain(t + 1)[way]
-
-                    @pl.when(go)
-                    def _():
-                        part_of = rg.at[slot, piece]
-                        remote(
-                            part_of, part_of, r_send.at[way, t + 1, e], r_recv.at[slot, e],
-                            to_row, col,
-                        ).start()
-
-    for n in range(1, steps):
-        spread_left(n)
+                    remote(
+                        part_of, part_of, r_send.at[way, t + 1, e], r_recv.at[slot, e],
+                        to_row, col,
+                    ).start()
+
+    def hops(first, last, urgent):
+
+        @pl.when(upward if urgent else jnp.logical_not(upward))
+        def _():
+            for t in range(first, last):
+                hop(t, 0)
+
+        @pl.when(jnp.logical_not(upward) if urgent else upward)
+        def _():
+            for t in range(first, last):
+                hop(t, 1)
+
+    ends = jnp.logical_or(row == 0, row == rn - 1)
+
+    @pl.when(is_home)
+    def _():
+        spread_left(0, True)
+
+    @pl.when(jnp.logical_and(is_home, ends))
+    def _():
+        for i in range(1, held):
+            spread_left(i, True)
+
+    @pl.when(jnp.logical_and(jnp.logical_not(is_home), ends))
+    def _():
+        for i in range(held):
+            spread_left(i, False)
+
+    hops(0, 1, True)
+
+    @pl.when(jnp.logical_and(is_home, jnp.logical_not(ends)))
+    def _():
+        for i in range(1, held):
+            spread_left(i, True)
+
+    hops(1, rn - 1, True)
+
+    @pl.when(jnp.logical_and(jnp.logical_not(is_home), jnp.logical_not(ends)))
+    def _():
+        for i in range(held):
+            spread_left(i, False)
+
+    hops(0, rn - 1, False)
+
     for g in range(rgroups):
-        slab = rg[:, g].astype(F32).reshape(depth, 128)
+        slab = rg[:, 1 + g].astype(F32).reshape(depth, 128)
         rt[g * 128 : (g + 1) * 128, :] = slab.T
     for q in range(pw):
         rq[q * cd : (q + 1) * cd, :] = rt[pl.ds(q, cd, stride=pw), :].astype(BF16)
 
     take_left(0)
     left_mask = lg[:, 0].astype(F32).reshape(depth, 128)
-    right_mask = rg[:, rgroups].astype(F32).reshape(depth, 128)
+    right_mask = rg[:, 0].astype(F32).reshape(depth, 128)
     counts = dot(right_mask.T.astype(BF16), left_mask.astype(BF16))
     inverse = 1.0 / jnp.maximum(counts, 1.0)
     for i in range(rd):
@@ -280,7 +343,9 @@
     def send_mirror(step, k, p):
         to_row, to_col = col * fold + k, row // fold
         mine = jnp.logical_and(to_row == row, to_col == col)
-        across = to_col // chans != col // chans
+        across = to_col // chans != chip
+        at_end = jnp.logical_or(to_row == 0, to_row == rn - 1)
+        turned = jnp.logical_and(across, at_end)
         src, dst = to_mirror(step, k, p)
         rsem = m_recv.at[row % fold, step, p]
         ssem = m_send.at[k, step, p]
@@ -289,51 +354,46 @@
         def _():
             pltpu.make_async_copy(src, dst, rsem).start()
 
-        direct = jnp.logical_not(mine)
-        if p == 1:
-            direct = jnp.logical_and(direct, jnp.logical_not(across))
-
-            @pl.when(across)
-            def _():
-                slot, core = to_row // chans, to_row % chans
-                remote(
-                    src, relay.at[slot, step], ssem, rl_recv.at[slot, step], row,
-                    to_col // chans * chans + core,
-                ).start()
-
-        @pl.when(direct)
+        @pl.when(turned)
+        def _():
+            slot = jnp.where(to_row == 0, 0, 1)
+            remote(
+                src, relay.at[slot, step, p], ssem, rl_recv.at[slot, step, p], row, to_col
+            ).start()
+
+        @pl.when(jnp.logical_not(jnp.logical_or(mine, turned)))
         def _():
             remote(src, dst, ssem, rsem, to_row, to_col).start()
 
-    def relayed(m):
-        key = m * chans + col % chans
-        from_col, to_row, to_col = key // fold, key, row // fold
-        active = jnp.logical_and(
-            to_col // chans == col // chans, from_col // chans != to_col // chans
-        )
-        return active, row, to_row, to_col
+    def relayed(slot):
+        to_row = (0, rn - 1)[slot]
+        active = jnp.logical_and(col == row // fold, to_row // fold // chans != chip)
+        return active, to_row
 
     def forward(step):
-        for m in range(rn // chans):
-            active, from_row, to_row, to_col = relayed(m)
+        for slot in range(2):
+            active, to_row = relayed(slot)
 
             @pl.when(active)
             def _():
-                piece = relay.at[m, step]
-                pltpu.make_async_copy(piece, piece, rl_recv.at[m, step]).wait()
-                begin = (from_row % fold) * rd + step * cr + part
-                remote(
-                    piece, mirror.at[pl.ds(begin, part)], rl_send.at[m, step],
-                    m_recv.at[from_row % fold, step, 1], to_row, to_col,
-                ).start()
-
-    lag = min(1, steps)
+                for p in (1, 0):
+                    piece = relay.at[slot, step, p]
+                    pltpu.make_async_copy(piece, piece, rl_recv.at[slot, step, p]).wait()
+                    begin = (row % fold) * rd + step * cr + p * part
+                    remote(
+                        piece, mirror.at[pl.ds(begin, part)], rl_send.at[slot, step, p],
+                        m_recv.at[row % fold, step, p], to_row, col,
+                    ).start()
 
     def one_step(step, carry):
 
         @pl.when(step > 0)
         def _():
             take_left(step)
+
+        @pl.when(2 * step < steps)
+        def _():
+            forward(2 * step)
 
         for g in range(cgroups):
             slab = lg[:, 1 + step * cgroups + g].astype(F32).reshape(depth, 128)
@@ -367,40 +427,76 @@
                 send_mirror(step, k, p)
             if p == 1:
 
-                @pl.when(step >= lag)
+                @pl.when(2 * step + 1 < steps)
                 def _():
-                    forward(step - lag)
+                    forward(2 * step + 1)
 
         return carry
 
     lax.fori_loop(0, steps, one_step, 0)
-    for step in range(steps - lag, steps):
-        forward(step)
-
-    for step in range(steps):
-        for k in range(fold):
-            begin = k * rd + step * cr
-            for p in (0, 1):
-                piece = mirror.at[pl.ds(begin + p * part, part)]
-                pltpu.make_async_copy(piece, piece, m_recv.at[k, step, p]).wait()
-            mf[begin * rd : (begin + cr) * rd, :] = (
-                mirror[begin : begin + cr].astype(F32).reshape(cr * rd, ch)
-            )
-            some_cols = valid_cols[begin : begin + cr]
-
-            def one_row(i, carry):
-                other = mf[pl.ds(begin * rd + i, cr, stride=rd), :]
-                half_sum = (two[i, begin : begin + cr].astype(F32) + other) * 0.5
-                sym[i, begin : begin + cr] = half_sum
-                masked = half_sum * some_cols * vrows[pl.ds(i, 1), :]
-                wide[i + 1, begin : begin + cr, ch : 2 * ch] = masked.astype(BF16)
-                if begin == 0:
-                    colf[0, pl.ds(i, 1), :] = masked[0:1]
-                if begin + cr == cd:
-                    colf[1, pl.ds(i, 1), :] = masked[cr - 1 : cr]
-                return carry
-
-            lax.fori_loop(0, rd, one_row, 0, unroll=4)
+
+    stripes = cd // cr
+    strip = min(32, rd)
+    place = lax.broadcasted_iota(jnp.int32, (cr, ch), 0)
+
+    def take_mirror(q):
+        begin = q * cr
+        k, step = begin // rd, begin % rd // cr
+        for p in (1, 0):
+            piece = mirror.at[pl.ds(begin + p * part, part)]
+            pltpu.make_async_copy(piece, piece, m_recv.at[k, step, p]).wait()
+        mf[begin * rd : (begin + cr) * rd, :] = (
+            mirror[begin : begin + cr].astype(F32).reshape(cr * rd, ch)
+        )
+        some_cols = valid_cols[begin : begin + cr]
+
+        def one_row(i, carry):
+            other = mf[pl.ds(begin * rd + i, cr, stride=rd), :]
+            half_sum = (two[i, begin : begin + cr].astype(F32) + other) * 0.5
+            sym[i, begin : begin + cr] = half_sum
+            masked = half_sum * some_cols * vrows[pl.ds(i, 1), :]
+            wide[i + 1, begin : begin + cr, ch : 2 * ch] = masked.astype(BF16)
+            before = colf[1, pl.ds(i, 1), :] if q else 0.0
+            wide[i + 1, begin : begin + cr, 0:ch] = jnp.where(
+                place == 0, before, pltpu.roll(masked, 1, 0)
+            ).astype(BF16)
+            if q:
+                earlier = wide[i + 1, begin - cr : begin, ch : 2 * ch].astype(F32)
+                wide[i + 1, begin - cr : begin, 2 * ch : 3 * ch] = jnp.where(
+                    place == cr - 1, masked[0:1], pltpu.roll(earlier, cr - 1, 0)
+                ).astype(BF16)
+            else:
+                colf[0, pl.ds(i, 1), :] = masked[0:1]
+            if q == stripes - 1:
+                wide[i + 1, begin : begin + cr, 2 * ch : 3 * ch] = jnp.where(
+                    place == cr - 1, 0.0, pltpu.roll(masked, cr - 1, 0)
+                ).astype(BF16)
+            colf[1, pl.ds(i, 1), :] = masked[cr - 1 : cr]
+            return carry
+
+        lax.fori_loop(0, rd, one_row, 0, unroll=4)
+
+    def conv(q):
+        begin = q * cr
+        for first in range(0, rd, strip):
+            total = sym[first : first + strip, begin : begin + cr].reshape(strip * cr, ch)
+            for a in range(3):
+                window = wide[first + a : first + a + strip, begin : begin + cr]
+                total = total + dot(window.reshape(strip * cr, 3 * ch), wk_ref[a])
+            total = total.reshape(strip, cr, ch)
+            out_ref[first : first + strip, begin : begin + cr] = total.astype(BF16)
+            if q in (0, stripes - 1):
+                sym[first : first + strip, begin : begin + cr] = total
+            else:
+                if first == 0:
+                    sym[0, begin : begin + cr] = total[0]
+                if first + strip == rd:
+                    sym[rd - 1, begin : begin + cr] = total[strip - 1]
+
+    for q in range(stripes):
+        take_mirror(q)
+        if 0 < q < stripes - 1:
+            conv(q - 1)
 
     for n, (a, b) in enumerate(AROUND):
         if b == 0:
@@ -430,20 +526,8 @@
                 h_recv.at[n], row + a, col + b,
             ).start()
 
-    place = lax.broadcasted_iota(jnp.int32, (cd, ch), 0)
-
-    def widen(i, before, after):
-        centre = wide[i, :, ch : 2 * ch].astype(F32)
-        wide[i, :, 0:ch] = jnp.where(place == 0, before, pltpu.roll(centre, 1, 0)).astype(BF16)
-        wide[i, :, 2 * ch : 3 * ch] = jnp.where(
-            place == cd - 1, after, pltpu.roll(centre, cd - 1, 0)
-        ).astype(BF16)
-
-    def widen_row(i, carry):
-        widen(i + 1, 0.0, 0.0)
-        return carry
-
-    lax.fori_loop(0, rd, widen_row, 0, unroll=4)
+    for q in range(max(stripes - 2, 0), stripes):
+        conv(q)
 
     for n, (a, b) in enumerate(AROUND):
 
@@ -453,46 +537,57 @@
             pltpu.make_async_copy(piece, piece, h_recv.at[n]).wait()
 
     slot_of = {direction: n for n, direction in enumerate(AROUND)}
-    wide[0, :, ch : 2 * ch] = hrecv[slot_of[(1, 0)], 0:cd]
-    wide[rd + 1, :, ch : 2 * ch] = hrecv[slot_of[(-1, 0)], 0:cd]
-    colf[0] = hrecv[slot_of[(0, 1)], 0:rd].astype(F32)
-    colf[1] = hrecv[slot_of[(0, -1)], 0:rd].astype(F32)
-    edge = lax.broadcasted_iota(jnp.int32, (16, ch), 0)
+    along = lax.broadcasted_iota(jnp.int32, (cd, ch), 0)
+    down = lax.broadcasted_iota(jnp.int32, (rd, ch), 0)
+
+    def edge_row(a, i):
+        line = hrecv[slot_of[(a, 0)], 0:cd]
+        centre = line.astype(F32)
+        before = hrecv[slot_of[(a, 1)], 0:16].astype(F32)[0:1]
+        after = hrecv[slot_of[(a, -1)], 0:16].astype(F32)[0:1]
+        lefts = jnp.where(along == 0, before, pltpu.roll(centre, 1, 0)).astype(BF16)
+        rights = jnp.where(along == cd - 1, after, pltpu.roll(centre, cd - 1, 0)).astype(BF16)
+        w = 0 if a > 0 else 2
+        sym[i] = sym[i] + (
+            dot(lefts, wk_ref[w, 0:ch])
+            + dot(line, wk_ref[w, ch : 2 * ch])
+            + dot(rights, wk_ref[w, 2 * ch : 3 * ch])
+        )
+
+    def edge_col(b):
+        line = hrecv[slot_of[(0, b)], 0:rd]
+        centre = line.astype(F32)
+        above = jnp.where(down == 0, 0.0, pltpu.roll(centre, 1, 0)).astype(BF16)
+        below = jnp.where(down == rd - 1, 0.0, pltpu.roll(centre, rd - 1, 0)).astype(BF16)
+        lo = 0 if b > 0 else 2 * ch
+        return (
+            dot(above, wk_ref[0, lo : lo + ch])
+            + dot(line, wk_ref[1, lo : lo + ch])
+            + dot(below, wk_ref[2, lo : lo + ch])
+        )
+
+    edge_row(1, 0)
+    edge_row(-1, rd - 1)
+    colf[0] = edge_col(1)
+    colf[1] = edge_col(-1)
+    for i in (0, rd - 1):
+        out_ref[i] = sym[i].astype(BF16)
 
     def patch_row(i, carry):
-        first = wide[i + 1, 0:16, 0:ch].astype(F32)
-        wide[i + 1, 0:16, 0:ch] = jnp.where(
-            edge == 0, colf[0, pl.ds(i, 1), :], first
+        first = sym[i, 0:16]
+        if cd == 16:
+            first = first + jnp.where(place16 == 15, colf[1, pl.ds(i, 1), :], 0.0)
+        out_ref[i, 0:16] = (
+            first + jnp.where(place16 == 0, colf[0, pl.ds(i, 1), :], 0.0)
         ).astype(BF16)
-        last = wide[i + 1, cd - 16 : cd, 2 * ch : 3 * ch].astype(F32)
-        wide[i + 1, cd - 16 : cd, 2 * ch : 3 * ch] = jnp.where(
-            edge == 15, colf[1, pl.ds(i, 1), :], last
-        ).astype(BF16)
+        if cd > 16:
+            out_ref[i, cd - 16 : cd] = (
+                sym[i, cd - 16 : cd] + jnp.where(place16 == 15, colf[1, pl.ds(i, 1), :], 0.0)
+            ).astype(BF16)
         return carry
 
+    place16 = lax.broadcasted_iota(jnp.int32, (16, ch), 0)
     lax.fori_loop(0, rd, patch_row, 0, unroll=4)
-    widen(
-        0,
-        hrecv[slot_of[(1, 1)], 0:16].astype(F32)[0:1],
-        hrecv[slot_of[(1, -1)], 0:16].astype(F32)[0:1],
-    )
-    widen(
-        rd + 1,
-        hrecv[slot_of[(-1, 1)], 0:16].astype(F32)[0:1],
-        hrecv[slot_of[(-1, -1)], 0:16].astype(F32)[0:1],
-    )
-
-    strip = 8
-
-    def conv(n, carry):
-        total = sym[pl.ds(n * strip, strip)].reshape(strip * cd, ch)
-        for a in range(3):
-            window = wide[pl.ds(n * strip + a, strip)].reshape(strip * cd, 3 * ch)
-            total = total + dot(window, wk_ref[a])
-        out_ref[pl.ds(n * strip, strip)] = total.astype(BF16).reshape(strip, cd, ch)
-        return carry
-
-    lax.fori_loop(0, rd // strip, conv, 0)
 
     for k in range(fold):
         @pl.when(jnp.logical_not(l1_target(k)[2]))
@@ -510,13 +605,14 @@
                     src, _dst = to_mirror(step, k, p)
                     pltpu.make_async_copy(src, src, m_send.at[k, step, p]).wait()
 
-    for m in range(rn // chans):
-
-        @pl.when(relayed(m)[0])
+    for slot in range(2):
+
+        @pl.when(relayed(slot)[0])
         def _():
             for step in range(steps):
-                piece = relay.at[m, step]
-                pltpu.make_async_copy(piece, piece, rl_send.at[m, step]).wait()
+                for p in (0, 1):
+                    piece = relay.at[slot, step, p]
+                    pltpu.make_async_copy(piece, piece, rl_send.at[slot, step, p]).wait()
 
     for t in range(rn - 1):
         for way, (go, slot, _to_row) in enumerate(chain(t)):
@@ -527,11 +623,20 @@
                     part_of = rg.at[slot, piece]
                     pltpu.make_async_copy(part_of, part_of, r_send.at[way, t, e]).wait()
 
-    for m in range(fold):
-        for d in range(1, cn):
+    for m in range(held):
+        for n in range(steps):
+            piece = lg.at[m * chans + core, span(n)]
+            for e in range(1, chans):
+                pltpu.make_async_copy(piece, piece, l2_send.at[m, e - 1, n]).wait()
+
+    @pl.when(is_home)
+    def _():
+        for m in range(held):
             for n in range(steps):
-                piece = lg.at[col + m * cn, span(n)]
-                pltpu.make_async_copy(piece, piece, l2_send.at[m, d - 1, n]).wait()
+                piece = lg.at[m * chans + core, span(n)]
+                for d in range(1, chips):
+                    pltpu.make_async_copy(piece, piece, x_send.at[m, d - 1, n]).wait()
+
     for n, (a, b) in enumerate(AROUND):
 
         @pl.when(there(a, b))
@@ -601,29 +706,35 @@
             pltpu.VMEM((8, tall, ch), BF16),
             pltpu.VMEM((8, tall, ch), BF16),
             dma((fold, steps)),
-            dma((fold, steps)),
-            dma((fold, cn - 1, steps)),
-            dma((fold, cn - 1, steps)),
-            dma((2, rn - 1, 2)),
-            dma((rn, 2)),
+            dma((rn // chans, steps)),
+            dma((rn // chans, max(cn // chans - 1, 1), steps)),
+            dma((rn // chans, max(chans - 1, 1), steps)),
+            dma((rn // chans, max(chans - 1, 1), steps)),
+            dma((2, rn - 1, min(4, cd // per))),
+            dma((rn, min(4, cd // per))),
             dma((fold, steps, 2)),
             dma((fold, steps, 2)),
-            pltpu.VMEM((rn // chans, steps, cr // 2, rd, ch), BF16),
-            dma((rn // chans, steps)),
-            dma((rn // chans, steps)),
+            pltpu.VMEM((2, steps, 2, cr // 2, rd, ch), BF16),
+            dma((2, steps, 2)),
+            dma((2, steps, 2)),
             dma((8,)),
             dma((8,)),
         ],
         compiler_params=pltpu.CompilerParams(
-            collective_id=0, has_side_effects=True, vmem_limit_bytes=60 * 1024 * 1024
+            collective_id=0, has_side_effects=True, vmem_limit_bytes=44 * 1024 * 1024
         ),
     )(
-        alignment_features,
-        alignment_mask,
-        token_valid.reshape(1, -1),
-        left_weight.T,
-        right_weight.T,
-        *large,
+        *[
+            pltpu.with_memory_space_constraint(value, pltpu.HBM)
+            for value in (
+                alignment_features,
+                alignment_mask,
+                token_valid.reshape(1, -1),
+                left_weight.T,
+                right_weight.T,
+                *large,
+            )
+        ]
     )
 
 

time: 64.1 us -> 58.5 us (0.913)
  Pallas kernels: 61.4 us -> 56.7 us
  local copies, waits for them, and re-layouts: 2.26 us -> 0.97 us
    pallas_call x1, Pallas kernels: 61.4 us -> 56.7 us  [on_device(): pl.pallas_call(functools.partial(block_kernel, sizes), out_shape=jax.Shap...]
    unnamed x1, local copies, waits for them, and re-layouts: 2.26 us -> 0.97 us
where the time goes in v1:
time: 58.5 us; the launch traced here: 57.7 us
  Pallas kernels  56.7 us (97%)
  local copies, waits for them, and re-layouts  0.97 us (2%)
    pallas_call x1, Pallas kernels, on_device(): pl.pallas_call(functools.partial(block_kernel, sizes), out_shape=jax.Shap...  56.7 us

profile of v1, /device:TPU:1, one launch (start us, length us, event | category | flops | bytes accessed | tf_op | source)
XLA Modules:
  0.0 57.7 jit_solution(5097449296789376401)
XLA Ops:
  0.0 56.7 %shard_map.109 = bf16[64,64,128]{2,1,0:T(8,128)(2,1)S(1)} custom-call(bf16[32,64,64]{2,1,0:T(8,128)(2,1)} %feat_ref.1, s32[32,64]{1,0:T(8,128)} %mask_ref.1, s32[1,256]{1,0:T(1,128)} %bitcast.7, bf16[32,64]{1,0:T(8,128)(2,1)} %bitcast.5, bf16[32,64]{1,0:T(8,128)(2,1)} %bitcast.6, bf16[64,64,128]{2,1,0:T(8,128)(2,1)} %rest_0_.1, bf16[1024,128]{1,0:T(8,128)(2,1)} %rest_1_.1, ...), custom_call_target="tpu_custom_call" | custom-call | tf_op jit(solution)/shard_map/pallas_call | solution.py:679
  56.7 1.0 %copy.13 = bf16[64,64,128]{2,1,0:T(8,128)(2,1)} copy(bf16[64,64,128]{2,1,0:T(8,128)(2,1)S(1)} %shard_map.109) | data formatting | bytes 2097152

commit v2 on v1

v2 whole, which is shorter than its diff:
```python
import functools

import jax
import jax.numpy as jnp
from jax import lax
from jax.experimental import pallas as pl
from jax.experimental.pallas import tpu as pltpu
from jax.sharding import PartitionSpec as P

epsilon = 1e-05
F32, BF16 = jnp.float32, jnp.bfloat16
MESH = pl.DeviceIdType.MESH
AROUND = [(a, b) for a in (-1, 0, 1) for b in (-1, 0, 1) if (a, b) != (0, 0)]


def dot(a, b):
    return jnp.dot(a, b, preferred_element_type=F32)


def block_kernel(sizes, *refs):
    far, (out_ref, *rest) = refs[:11], refs[11:]
    near, (w_sem, *rest) = rest[:11], rest[11:]
    feat_ref, mask_ref, valid_ref, wl_ref, wr_ref = near[:5]
    pair_ref, wo_ref, wg_ref, wu_ref, wd_ref, wk_ref = near[5:]
    (
    proj,
    vrows,
    lsend,
    lg,
    rg,
    rt,
    rq,
    lcat,
    wof,
    w2,
    zs,
    rexp,
    inv,
    ones,
    two,
    mirror,
    mf,
    sym,
    wide,
    colf,
    hsend,
    hrecv,
    result,
    l1_send,
    l1_recv,
    x_send,
    l2_send,
    l2_recv,
    r_send,
    r_recv,
    m_send,
    m_recv,
    relay,
    rl_send,
    rl_recv,
    h_send,
    h_recv,
    o_sem,
    ) = rest
    rn, cn, chans, fold, rd, cd, ch, sl, tl, pw, cr = sizes
    row = lax.axis_index("row")
    col = lax.axis_index("col") * chans + lax.axis_index("chan")
    per = 128 // pw
    lgroups, rgroups = rd // per, cd // per
    cuts = min(4, rgroups)
    depth = rn * sl
    steps = rd // cr
    cgroups = cr // per
    half = cd // 2
    seg = min(half, rd)
    subs = rd // seg

    def at(r, c):
        return {"row": r, "col": c // chans, "chan": c % chans}

    def remote(src, dst, ssem, rsem, r, c):
        return pltpu.make_async_remote_copy(
            src_ref=src, dst_ref=dst, send_sem=ssem, recv_sem=rsem,
            device_id=at(r, c), device_id_type=MESH,
        )

    loads = [pltpu.make_async_copy(far[n], near[n], w_sem.at[n]) for n in range(11)]
    for n in (0, 1, 3, 4, 2, 6, 5, 7, 8, 9, 10):
        loads[n].start()
    barrier = pltpu.get_barrier_semaphore()

    def greet(n, carry):
        pl.semaphore_signal(barrier, inc=1, device_id=at(n // cn, n % cn), device_id_type=MESH)
        return carry

    lax.fori_loop(0, rn * cn, greet, 0)
    hrecv[...] = jnp.zeros_like(hrecv)
    for i in (0, rd + 1):
        wide[i] = jnp.zeros((cd, 3 * ch), BF16)

    spread = (
        lax.broadcasted_iota(jnp.int32, (pw, 128), 1) % pw
        == lax.broadcasted_iota(jnp.int32, (pw, 128), 0)
    ).astype(F32).astype(BF16)
    for n in (0, 1, 3, 4):
        loads[n].wait()
    mask = mask_ref[...].astype(F32).astype(BF16)
    spots = tl // per
    token_of = (
        lax.broadcasted_iota(jnp.int32, (tl, spots * 128), 1) // pw
        == lax.broadcasted_iota(jnp.int32, (tl, spots * 128), 0)
    ).astype(F32).astype(BF16)
    wide_mask = dot(mask, token_of)
    feats = feat_ref[...].reshape(sl * tl, feat_ref.shape[2])
    lane_of = lax.broadcasted_iota(jnp.int32, (sl, 128), 1) // pw

    def project(n, w_ref):
        tiled = lax.dot_general(
            w_ref[...], spread, (((0,), (0,)), ((), ())), preferred_element_type=F32
        ).astype(BF16)
        proj[n] = dot(feats, tiled)
        parts = []
        for g in range(spots):
            got = proj[n, pl.ds(g * per, sl, stride=tl), :]
            for t in range(1, per):
                other = proj[n, pl.ds(g * per + t, sl, stride=tl), :]
                got = jnp.where(lane_of == t, other, got)
            parts.append((got * wide_mask[:, g * 128 : (g + 1) * 128]).astype(BF16))
        return parts

    left = project(0, wl_ref)
    for k in range(fold):
        for g in range(lgroups):
            lsend[k, 1 + g] = left[k * lgroups + g]
        lsend[k, 0] = jnp.zeros((sl, 128), BF16)
        lsend[k, 0, :, 0:rd] = mask[:, k * rd : (k + 1) * rd]
    def project_right():
        right = project(1, wr_ref)
        for g in range(rgroups):
            rg[row, 1 + g] = right[g]
        rg[row, 0] = jnp.zeros((sl, 128), BF16)
        rg[row, 0, :, 0:tl] = mask

    early = row < rn // 2

    @pl.when(early)
    def _():
        project_right()


    pl.semaphore_wait(barrier, rn * cn)

    def span(n):
        if isinstance(n, int) and n == 0:
            return pl.ds(0, cgroups + 1)
        return pl.ds(1 + n * cgroups, cgroups)

    core, chip = col % chans, col // chans
    held = rn // chans
    home = row // fold // chans
    is_home = chip == home

    def l1_target(k):
        to_row, to_col = col * fold + k, chip * chans + row % chans
        return to_row, to_col, jnp.logical_and(to_row == row, to_col == col)

    def send_left(n):
        for k in range(fold):
            to_row, to_col, mine = l1_target(k)
            slot = row // chans
            src, dst = lsend.at[k, span(n)], lg.at[row, span(n)]

            @pl.when(mine)
            def _():
                pltpu.make_async_copy(src, dst, l1_recv.at[slot, n]).start()

            @pl.when(jnp.logical_not(mine))
            def _():
                remote(src, dst, l1_send.at[k, n], l1_recv.at[slot, n], to_row, to_col).start()

    chips = cn // chans

    def spread_left(i, n, at_home):
        m = (row // chans + i) % held
        piece = lg.at[m * chans + core, span(n)]
        pltpu.make_async_copy(piece, piece, l1_recv.at[m, n]).wait()
        if at_home:
            for d in range(1, chips):
                remote(
                    piece, piece, x_send.at[m, d - 1, n], l1_recv.at[m, n],
                    row, (chip + d) % chips * chans + core,
                ).start()
        for e in range(1, chans):
            remote(
                piece, piece, l2_send.at[m, e - 1, n], l2_recv.at[m, e - 1, n],
                row, chip * chans + (core + e) % chans,
            ).start()

    def take_left(n):
        for m in range(held):
            for e in range(1, chans):
                piece = lg.at[m * chans + (core + chans - e) % chans, span(n)]
                pltpu.make_async_copy(piece, piece, l2_recv.at[m, e - 1, n]).wait()

    send_left(0)

    @pl.when(jnp.logical_not(early))
    def _():
        project_right()

    def chain(t):
        low, high = jnp.maximum(row - t, 0), jnp.minimum(row + t, rn - 1)
        ups = jnp.logical_and(row - t >= 0, row + 1 < rn)
        downs = jnp.logical_and(row + t < rn, row >= 1)
        return (ups, low, row + 1), (downs, high, row - 1)

    quarter = rgroups // cuts
    pieces = [
        pl.ds(1 + e * quarter, quarter) if e else pl.ds(0, 1 + quarter) for e in range(cuts)
    ]

    upward = chip < chips // 2

    def pass_on(urgent, later):
        for way, (go, slot, to_row) in enumerate(chain(0)):

            @pl.when(jnp.logical_and(go, upward == (urgent == (way == 0))))
            def _():
                for e in cut_range(later):
                    part_of = rg.at[slot, pieces[e]]
                    remote(
                        part_of, part_of, r_send.at[way, 0, e], r_recv.at[slot, e], to_row, col
                    ).start()

    def cut_range(later):
        return range(cuts // 2, cuts) if later else range(cuts // 2)

    pass_on(True, False)
    pass_on(False, False)
    for n in range(1, steps):
        send_left(n)

    loads[2].wait()
    tokens = valid_ref.shape[1]
    valid = valid_ref[...].astype(F32)

    def as_rows(first, count):
        hit = lax.broadcasted_iota(jnp.int32, (count, tokens), 1) == first + (
            lax.broadcasted_iota(jnp.int32, (count, tokens), 0)
        )
        chosen = jnp.where(hit, jnp.broadcast_to(valid, (count, tokens)), 0.0).astype(BF16)
        return dot(chosen, jnp.ones((tokens, ch), BF16))

    vrows[0:rd] = as_rows(row * rd, rd)
    valid_cols = as_rows(col * cd, cd)

    loads[6].wait()
    wof[...] = wo_ref[...].astype(F32)
    w2[...] = jnp.zeros_like(w2)
    for q in range(pw):
        values = wof[pl.ds(q, pw, stride=pw), :].astype(BF16)
        for i in range(2):
            begin = q // 2 * 128 + (q % 2 * 2 + i) * pw
            w2[begin : begin + pw, i * ch : (i + 1) * ch] = values

    def hop(t, way, later):
        there_is, slot = (
            (row - t - 1 >= 0, jnp.maximum(row - t - 1, 0)),
            (row + t + 1 < rn, jnp.minimum(row + t + 1, rn - 1)),
        )[way]
        for e in cut_range(later):
            piece = pieces[e]

            @pl.when(there_is)
            def _():
                part_of = rg.at[slot, piece]
                pltpu.make_async_copy(part_of, part_of, r_recv.at[slot, e]).wait()

            if t + 1 < rn - 1:
                go, _slot, to_row = chain(t + 1)[way]

                @pl.when(go)
                def _():
                    part_of = rg.at[slot, piece]
                    remote(
                        part_of, part_of, r_send.at[way, t + 1, e], r_recv.at[slot, e],
                        to_row, col,
                    ).start()

    def hops(first, last, urgent, later=False):

        @pl.when(upward if urgent else jnp.logical_not(upward))
        def _():
            for t in range(first, last):
                hop(t, 0, later)

        @pl.when(jnp.logical_not(upward) if urgent else upward)
        def _():
            for t in range(first, last):
                hop(t, 1, later)

    ends = jnp.logical_or(row == 0, row == rn - 1)
    inner = jnp.logical_not(ends)
    away = jnp.logical_not(is_home)

    @pl.when(is_home)
    def _():
        spread_left(0, 0, True)

    @pl.when(jnp.logical_and(is_home, ends))
    def _():
        for i in range(1, held):
            spread_left(i, 0, True)

    @pl.when(jnp.logical_and(away, ends))
    def _():
        for i in range(held):
            spread_left(i, 0, False)

    hops(0, 1, True)
    pass_on(True, True)

    @pl.when(ends)
    def _():
        pass_on(False, True)


    @pl.when(jnp.logical_and(is_home, inner))
    def _():
        for i in range(1, held):
            spread_left(i, 0, True)

    hops(1, rn - 1, True)

    @pl.when(jnp.logical_and(away, inner))
    def _():
        for i in range(held):
            spread_left(i, 0, False)

    @pl.when(is_home)
    def _():
        for n in range(1, steps):
            for i in range(held):
                spread_left(i, n, True)

    @pl.when(is_home)
    def _():
        hops(0, 1, True, True)

    hops(0, rn - 1, False)

    @pl.when(inner)
    def _():
        pass_on(False, True)

    take_left(0)
    left_mask = lg[:, 0].astype(F32).reshape(depth, 128)
    right_mask = rg[:, 0].astype(F32).reshape(depth, 128)
    counts = dot(right_mask.T.astype(BF16), left_mask.astype(BF16))
    inv[...] = 1.0 / jnp.maximum(counts, 1.0)

    def prepare(h):
        for g in range(h * rgroups // 2, (h + 1) * rgroups // 2):
            slab = rg[:, 1 + g].astype(F32).reshape(depth, 128)
            rt[g * 128 : (g + 1) * 128, :] = slab.T
        for q in range(pw):
            rq[h, q // 2 * half : (q // 2 + 1) * half, q % 2 * depth : (q % 2 + 1) * depth] = rt[
                pl.ds(h * half * pw + q, half, stride=pw), :
            ].astype(BF16)
        inverse = inv[h * half : (h + 1) * half]
        for i in range(rd):
            rexp[i, h * half : (h + 1) * half] = jnp.broadcast_to(
                inverse[:, i : i + 1], (half, ch)
            )

    prepare(0)

    for n in (5, 7, 8, 9, 10):
        loads[n].wait()

    lag = 0

    def segments(h):
        found = []
        for begin in range(h * half, (h + 1) * half, seg):
            found.append((begin, begin // rd, begin % rd))
        return found

    def send_mirror(h, step):
        for begin, k, off in segments(h):
            to_row, to_col = col * fold + k, row // fold
            mine = jnp.logical_and(to_row == row, to_col == col)
            across = to_col // chans != chip
            at_end = jnp.logical_or(to_row == 0, to_row == rn - 1)
            turned = jnp.logical_and(across, at_end)
            sub = off // seg
            src = two.at[pl.ds(step * cr, cr), pl.ds(begin, seg)]
            dst = mirror.at[pl.ds(row % fold * rd + step * cr, cr), pl.ds(off, seg)]
            rsem = m_recv.at[row % fold, step, sub]
            ssem = m_send.at[k, step, sub]

            @pl.when(mine)
            def _():
                pltpu.make_async_copy(src, dst, rsem).start()

            @pl.when(turned)
            def _():
                slot = jnp.where(to_row == 0, 0, 1)
                remote(
                    src, relay.at[slot, step, sub], ssem, rl_recv.at[slot, step, sub],
                    row, to_col,
                ).start()

            @pl.when(jnp.logical_not(jnp.logical_or(mine, turned)))
            def _():
                remote(src, dst, ssem, rsem, to_row, to_col).start()

    def relayed(slot):
        to_row = (0, rn - 1)[slot]
        active = jnp.logical_and(col == row // fold, to_row // fold // chans != chip)
        return active, to_row

    def forward(h, step):
        for slot in range(2):
            active, to_row = relayed(slot)
            for _begin, k, off in segments(h):
                if k == to_row % fold:
                    sub = off // seg

                    @pl.when(active)
                    def _():
                        piece = relay.at[slot, step, sub]
                        pltpu.make_async_copy(piece, piece, rl_recv.at[slot, step, sub]).wait()
                        remote(
                            piece,
                            mirror.at[pl.ds(row % fold * rd + step * cr, cr), pl.ds(off, seg)],
                            rl_send.at[slot, step, sub],
                            m_recv.at[row % fold, step, sub], to_row, col,
                        ).start()

    low_lanes = lax.broadcasted_iota(jnp.int32, (depth, 128), 1) < 64

    def serve(step):
        for t in range(rn - 1):

            @pl.when(step == min(t, steps - 1))
            def _():
                for way in (0, 1):
                    if t:
                        hop(t, way, True)
                    else:

                        @pl.when(jnp.logical_or(away, upward == (way == 1)))
                        def _():
                            hop(0, way, True)

        @pl.when(jnp.logical_and(away, step + 1 < steps))
        def _():
            for i in range(held):
                spread_left(i, step + 1, False)

        @pl.when(step > 0)
        def _():
            take_left(step)

    def one_step(h, step):
        lo = h * half
        if h == 0:
            serve(step)

        @pl.when(step >= lag)
        def _():
            forward(h, step - lag)

        if h and lag:

            @pl.when(step < lag)
            def _():
                forward(h - 1, steps - lag + step)

        for g in range(cgroups):
            slab = lg[:, 1 + step * cgroups + g].astype(F32).reshape(depth, 128)
            turned = pltpu.roll(slab, 64, 1)
            for i, (first, second) in enumerate(((slab, turned), (turned, slab))):
                at_lane = (g * 2 + i) * 128
                lcat[0:depth, at_lane : at_lane + 128] = jnp.where(low_lanes, first, 0.0).astype(BF16)
                lcat[depth : 2 * depth, at_lane : at_lane + 128] = jnp.where(
                    low_lanes, 0.0, second
                ).astype(BF16)
        for g in range(cgroups):
            z = dot(rq[h], lcat[:, g * 256 : (g + 1) * 256]).astype(BF16)
            for i in range(2):
                for q in range(pw // 2):
                    begin = (i * cgroups + g) * half
                    zs[begin : begin + half, q * 128 : (q + 1) * 128] = z[
                        q * half : (q + 1) * half, i * 128 : (i + 1) * 128
                    ]
        update = dot(zs[...], w2[...])
        for g in range(cgroups):
            for i in range(per):
                at_row = step * cr + g * per + i
                begin = (i // 2 * cgroups + g) * half
                add = update[begin : begin + half, i % 2 * ch : (i % 2 + 1) * ch]
                add = add * rexp[at_row, lo : lo + half]
                ones[g * per + i] = (pair_ref[at_row, lo : lo + half].astype(F32) + add).astype(BF16)
        values = ones[...].reshape(cr * half, ch).astype(F32)
        centre = jnp.mean(values, axis=-1, keepdims=True)
        shifted = values - centre
        var = jnp.mean(jnp.square(shifted), axis=-1, keepdims=True)
        normed = (shifted * lax.rsqrt(var + epsilon)).astype(BF16)
        gate = dot(normed, wg_ref[...])
        up = dot(normed, wu_ref[...])
        hidden = (gate / (1.0 + jnp.exp(-gate)) * up).astype(BF16)
        done = (values + dot(hidden, wd_ref[...])).astype(BF16)
        two[pl.ds(step * cr, cr), lo : lo + half] = done.reshape(cr, half, ch)
        send_mirror(h, step)

    def run(h):
        def body(step, carry):
            one_step(h, step)
            return carry

        lax.fori_loop(0, steps, body, 0)

    run(0)
    prepare(1)
    run(1)
    for step in range(steps - lag, steps):
        forward(1, step)

    stripes = cd // cr
    place = lax.broadcasted_iota(jnp.int32, (cr, ch), 0)

    def take_mirror(sub, q):
        begin = q * cr
        k, step = begin // rd, begin % rd // cr
        top = sub * seg
        piece = mirror.at[pl.ds(begin, cr), pl.ds(top, seg)]
        pltpu.make_async_copy(piece, piece, m_recv.at[k, step, sub]).wait()
        mf[0 : cr * seg] = (
            mirror[begin : begin + cr, top : top + seg].astype(F32).reshape(cr * seg, ch)
        )
        some_cols = valid_cols[begin : begin + cr]

        def one_row(i, carry):
            other = mf[pl.ds(i - top, cr, stride=seg), :]
            half_sum = (two[i, begin : begin + cr].astype(F32) + other) * 0.5
            sym[i, begin : begin + cr] = half_sum
            masked = half_sum * some_cols * vrows[pl.ds(i, 1), :]
            wide[i + 1, begin : begin + cr, ch : 2 * ch] = masked.astype(BF16)
            before = colf[1, pl.ds(i, 1), :] if q else 0.0
            wide[i + 1, begin : begin + cr, 0:ch] = jnp.where(
                place == 0, before, pltpu.roll(masked, 1, 0)
            ).astype(BF16)
            if q:
                earlier = wide[i + 1, begin - cr : begin, ch : 2 * ch].astype(F32)
                wide[i + 1, begin - cr : begin, 2 * ch : 3 * ch] = jnp.where(
                    place == cr - 1, masked[0:1], pltpu.roll(earlier, cr - 1, 0)
                ).astype(BF16)
            else:
                colf[0, pl.ds(i, 1), :] = masked[0:1]
            if q == stripes - 1:
                wide[i + 1, begin : begin + cr, 2 * ch : 3 * ch] = jnp.where(
                    place == cr - 1, 0.0, pltpu.roll(masked, cr - 1, 0)
                ).astype(BF16)
            colf[1, pl.ds(i, 1), :] = masked[cr - 1 : cr]
            return carry

        lax.fori_loop(top, top + seg, one_row, 0, unroll=4)

    strip = min(32, rd)

    def conv(q):
        begin = q * cr
        for first in range(0, rd, strip):
            total = sym[first : first + strip, begin : begin + cr].reshape(strip * cr, ch)
            for a in range(3):
                window = wide[first + a : first + a + strip, begin : begin + cr]
                total = total + dot(window.reshape(strip * cr, 3 * ch), wk_ref[a])
            total = total.reshape(strip, cr, ch)
            result[first : first + strip, begin : begin + cr] = total.astype(BF16)
            if q in (0, stripes - 1):
                sym[first : first + strip, begin : begin + cr] = total
            else:
                if first == 0:
                    sym[0, begin : begin + cr] = total[0]
                if first + strip == rd:
                    sym[rd - 1, begin : begin + cr] = total[strip - 1]
        if 0 < q < stripes - 1:
            middle(q).start()

    def middle(q):
        block = (pl.ds(1, rd - 2), pl.ds(q * cr, cr))
        return pltpu.make_async_copy(result.at[block], out_ref.at[block], o_sem.at[0, q])

    for sub in range(subs):
        for q in range(stripes):
            take_mirror(sub, q)
            if sub == subs - 1 and 0 < q < stripes - 1:
                conv(q - 1)

    for n, (a, b) in enumerate(AROUND):
        if b == 0:
            hsend[n, 0:cd] = wide[1 if a < 0 else rd, :, ch : 2 * ch]
        elif a == 0:
            hsend[n, 0:rd] = colf[0 if b < 0 else 1].astype(BF16)
        else:
            corner = colf[0 if b < 0 else 1, 0:1] if a < 0 else colf[0 if b < 0 else 1, rd - 1 : rd]
            hsend[n, 0:16] = jnp.broadcast_to(corner, (16, ch)).astype(BF16)

    def there(a, b):
        r, c = row + a, col + b
        return jnp.logical_and(
            jnp.logical_and(r >= 0, r < rn), jnp.logical_and(c >= 0, c < cn)
        )

    def lines(a, b):
        return cd if b == 0 else (rd if a == 0 else 16)

    for n, (a, b) in enumerate(AROUND):

        @pl.when(there(a, b))
        def _():
            size = lines(a, b)
            remote(
                hsend.at[n, pl.ds(0, size)], hrecv.at[n, pl.ds(0, size)], h_send.at[n],
                h_recv.at[n], row + a, col + b,
            ).start()

    for q in range(max(stripes - 2, 0), stripes):
        conv(q)

    for n, (a, b) in enumerate(AROUND):

        @pl.when(there(-a, -b))
        def _():
            piece = hrecv.at[n, pl.ds(0, lines(a, b))]
            pltpu.make_async_copy(piece, piece, h_recv.at[n]).wait()

    slot_of = {direction: n for n, direction in enumerate(AROUND)}
    along = lax.broadcasted_iota(jnp.int32, (cd, ch), 0)
    down = lax.broadcasted_iota(jnp.int32, (rd, ch), 0)

    def edge_row(a, i):
        line = hrecv[slot_of[(a, 0)], 0:cd]
        centre = line.astype(F32)
        before = hrecv[slot_of[(a, 1)], 0:16].astype(F32)[0:1]
        after = hrecv[slot_of[(a, -1)], 0:16].astype(F32)[0:1]
        lefts = jnp.where(along == 0, before, pltpu.roll(centre, 1, 0)).astype(BF16)
        rights = jnp.where(along == cd - 1, after, pltpu.roll(centre, cd - 1, 0)).astype(BF16)
        w = 0 if a > 0 else 2
        sym[i] = sym[i] + (
            dot(lefts, wk_ref[w, 0:ch])
            + dot(line, wk_ref[w, ch : 2 * ch])
            + dot(rights, wk_ref[w, 2 * ch : 3 * ch])
        )

    def edge_col(b):
        line = hrecv[slot_of[(0, b)], 0:rd]
        centre = line.astype(F32)
        above = jnp.where(down == 0, 0.0, pltpu.roll(centre, 1, 0)).astype(BF16)
        below = jnp.where(down == rd - 1, 0.0, pltpu.roll(centre, rd - 1, 0)).astype(BF16)
        lo = 0 if b > 0 else 2 * ch
        return (
            dot(above, wk_ref[0, lo : lo + ch])
            + dot(line, wk_ref[1, lo : lo + ch])
            + dot(below, wk_ref[2, lo : lo + ch])
        )

    edge_row(1, 0)
    edge_row(-1, rd - 1)
    colf[0] = edge_col(1)
    colf[1] = edge_col(-1)
    for i in (0, rd - 1):
        result[i] = sym[i].astype(BF16)

    def patch_row(i, carry):
        first = sym[i, 0:16]
        if cd == 16:
            first = first + jnp.where(place16 == 15, colf[1, pl.ds(i, 1), :], 0.0)
        result[i, 0:16] = (
            first + jnp.where(place16 == 0, colf[0, pl.ds(i, 1), :], 0.0)
        ).astype(BF16)
        if cd > 16:
            result[i, cd - 16 : cd] = (
                sym[i, cd - 16 : cd] + jnp.where(place16 == 15, colf[1, pl.ds(i, 1), :], 0.0)
            ).astype(BF16)
        return carry

    place16 = lax.broadcasted_iota(jnp.int32, (16, ch), 0)
    lax.fori_loop(0, rd, patch_row, 0, unroll=4)

    closing = []
    for n, i in enumerate((0, rd - 1)):
        closing.append(pltpu.make_async_copy(result.at[i], out_ref.at[i], o_sem.at[1, n]))
    for n, q in enumerate((0, stripes - 1)):
        block = (pl.ds(1, rd - 2), pl.ds(q * cr, cr))
        closing.append(
            pltpu.make_async_copy(result.at[block], out_ref.at[block], o_sem.at[2, n])
        )
    for copy in closing:
        copy.start()

    for k in range(fold):
        @pl.when(jnp.logical_not(l1_target(k)[2]))
        def _():
            for n in range(steps):
                piece = lsend.at[k, span(n)]
                pltpu.make_async_copy(piece, piece, l1_send.at[k, n]).wait()

        to_row, to_col = col * fold + k, row // fold

        @pl.when(jnp.logical_not(jnp.logical_and(to_row == row, to_col == col)))
        def _():
            for step in range(steps):
                for sub in range(subs):
                    src = two.at[pl.ds(step * cr, cr), pl.ds(k * rd + sub * seg, seg)]
                    pltpu.make_async_copy(src, src, m_send.at[k, step, sub]).wait()

    for slot in range(2):

        @pl.when(relayed(slot)[0])
        def _():
            for step in range(steps):
                for sub in range(subs):
                    piece = relay.at[slot, step, sub]
                    pltpu.make_async_copy(piece, piece, rl_send.at[slot, step, sub]).wait()

    for t in range(rn - 1):
        for way, (go, slot, _to_row) in enumerate(chain(t)):

            @pl.when(go)
            def _():
                for e, piece in enumerate(pieces):
                    part_of = rg.at[slot, piece]
                    pltpu.make_async_copy(part_of, part_of, r_send.at[way, t, e]).wait()

    for m in range(held):
        for n in range(steps):
            piece = lg.at[m * chans + core, span(n)]
            for e in range(1, chans):
                pltpu.make_async_copy(piece, piece, l2_send.at[m, e - 1, n]).wait()

    @pl.when(is_home)
    def _():
        for m in range(held):
            for n in range(steps):
                piece = lg.at[m * chans + core, span(n)]
                for d in range(1, chips):
                    pltpu.make_async_copy(piece, piece, x_send.at[m, d - 1, n]).wait()

    for n, (a, b) in enumerate(AROUND):

        @pl.when(there(a, b))
        def _():
            piece = hsend.at[n, pl.ds(0, lines(a, b))]
            pltpu.make_async_copy(piece, piece, h_send.at[n]).wait()
    for q in range(1, stripes - 1):
        middle(q).wait()
    for copy in closing:
        copy.wait()


def on_device(
    mesh_shape,
    pair_input,
    alignment_features,
    alignment_mask,
    token_valid,
    left_weight,
    right_weight,
    output_weight,
    gate_weight,
    up_weight,
    down_weight,
    kernel_weight,
):
    rd, cd, ch = pair_input.shape
    sl, tl, aw = alignment_features.shape
    pw = left_weight.shape[1]
    hid = gate_weight.shape[1]
    rn, chans = mesh_shape["row"], mesh_shape["chan"]
    cn = mesh_shape["col"] * chans
    fold = rn // cn
    per = 128 // pw
    cr = min(16, rd)
    depth = rn * sl
    steps = rd // cr
    tall = max(rd, cd, 16)
    half = cd // 2
    seg = min(half, rd)
    subs = rd // seg
    groups, rgroups = rd // per, cd // per
    cuts = min(4, rgroups)
    held = rn // chans
    sizes = (rn, cn, chans, fold, rd, cd, ch, sl, tl, pw, cr)
    operands = (
        alignment_features,
        alignment_mask,
        token_valid.reshape(1, -1),
        left_weight.T,
        right_weight.T,
        pair_input,
        output_weight,
        gate_weight,
        up_weight,
        down_weight,
        kernel_weight.reshape(3, 3 * ch, ch),
    )
    dma = pltpu.SemaphoreType.DMA
    anywhere = pl.BlockSpec(memory_space=pl.ANY)
    return pl.pallas_call(
        functools.partial(block_kernel, sizes),
        out_shape=jax.ShapeDtypeStruct((rd, cd, ch), BF16),
        in_specs=[anywhere] * len(operands),
        out_specs=anywhere,
        scratch_shapes=[
            *[pltpu.VMEM(value.shape, value.dtype) for value in operands],
            dma((len(operands),)),
            pltpu.VMEM((2, sl * tl, 128), F32),
            pltpu.VMEM((tall, ch), F32),
            pltpu.VMEM((fold, groups + 1, sl, 128), BF16),
            pltpu.VMEM((rn, groups + 1, sl, 128), BF16),
            pltpu.VMEM((rn, rgroups + 1, sl, 128), BF16),
            pltpu.VMEM((cd * pw, depth), F32),
            pltpu.VMEM((2, pw // 2 * half, 2 * depth), BF16),
            pltpu.VMEM((2 * depth, cr * pw * 2), BF16),
            pltpu.VMEM((pw * pw, ch), F32),
            pltpu.VMEM((pw // 2 * 128, 2 * ch), BF16),
            pltpu.VMEM((2 * (cr // per) * half, pw // 2 * 128), BF16),
            pltpu.VMEM((rd, cd, ch), F32),
            pltpu.VMEM((128, 128), F32),
            pltpu.VMEM((cr, half, ch), BF16),
            pltpu.VMEM((rd, cd, ch), BF16),
            pltpu.VMEM((cd, rd, ch), BF16),
            pltpu.VMEM((cr * seg, ch), F32),
            pltpu.VMEM((rd, cd, ch), F32),
            pltpu.VMEM((rd + 2, cd, 3 * ch), BF16),
            pltpu.VMEM((2, rd, ch), F32),
            pltpu.VMEM((8, tall, ch), BF16),
            pltpu.VMEM((8, tall, ch), BF16),
            pltpu.VMEM((rd, cd, ch), BF16),
            dma((fold, steps)),
            dma((held, steps)),
            dma((held, max(cn // chans - 1, 1), steps)),
            dma((held, max(chans - 1, 1), steps)),
            dma((held, max(chans - 1, 1), steps)),
            dma((2, rn - 1, cuts)),
            dma((rn, cuts)),
            dma((fold, steps, subs)),
            dma((fold, steps, subs)),
            pltpu.VMEM((2, steps, subs, cr, seg, ch), BF16),
            dma((2, steps, subs)),
            dma((2, steps, subs)),
            dma((8,)),
            dma((8,)),
            dma((3, max(cd // cr, 2))),
        ],
        compiler_params=pltpu.CompilerParams(
            collective_id=0, has_side_effects=True, vmem_limit_bytes=44 * 1024 * 1024
        ),
    )(*[pltpu.with_memory_space_constraint(value, pltpu.HBM) for value in operands])


def solution(mesh):
    placed = (
        P(("groups", "row"), ("col", "chan"), None),
        P("row", ("groups", "col", "chan"), None),
        P("row", ("groups", "col", "chan")),
        P("groups"),
        P(),
        P(),
        P(),
        P(),
        P(),
        P(),
        P(),
    )
    return jax.shard_map(
        functools.partial(on_device, dict(mesh.shape)),
        mesh=mesh,
        in_specs=placed,
        out_specs=P(("groups", "row"), ("col", "chan"), None),
        check_vma=False,
    )
```

time: 58.5 us -> 52.8 us (0.903); the launches traced: 57.7 us -> 52.7 us
  Pallas kernels: 56.7 us -> 51.7 us
    pallas_call x1, Pallas kernels: 56.7 us -> 51.7 us  [on_device(): pl.pallas_call(functools.partial(block_kernel, sizes), out_shape=jax.Shap...]
where the time goes in v2:
time: 52.8 us; the launch traced here: 52.7 us
  Pallas kernels  51.7 us (98%)
  local copies, waits for them, and re-layouts  0.97 us (2%)
    pallas_call x1, Pallas kernels, on_device(): pl.pallas_call(functools.partial(block_kernel, sizes), out_shape=jax.Shap...  51.7 us

profile of v2, /device:TPU:1, one launch (start us, length us, event | category | flops | bytes accessed | tf_op | source)
XLA Modules:
  0.0 52.7 jit_solution(4076833605823689931)
XLA Ops:
  0.0 51.7 %shard_map.109 = bf16[64,64,128]{2,1,0:T(8,128)(2,1)S(1)} custom-call(bf16[32,64,64]{2,1,0:T(8,128)(2,1)} %refs_0_.1, s32[32,64]{1,0:T(8,128)} %refs_1_.1, s32[1,256]{1,0:T(1,128)} %bitcast.7, bf16[32,64]{1,0:T(8,128)(2,1)} %bitcast.5, bf16[32,64]{1,0:T(8,128)(2,1)} %bitcast.6, bf16[64,64,128]{2,1,0:T(8,128)(2,1)} %refs_5_.1, bf16[1024,128]{1,0:T(8,128)(2,1)} %refs_6_.1, ...), custom_call_target="tpu_custom_call" | custom-call | tf_op jit(solution)/shard_map/pallas_call | solution.py:812
  51.7 1.0 %copy.13 = bf16[64,64,128]{2,1,0:T(8,128)(2,1)} copy(bf16[64,64,128]{2,1,0:T(8,128)(2,1)S(1)} %shard_map.109) | data formatting | bytes 2097152

commit v3 on v2

--- a/solution.py
+++ b/solution.py
@@ -49,6 +49,7 @@
     l1_send,
     l1_recv,
     x_send,
+    e_send,
     l2_send,
     l2_recv,
     r_send,
@@ -67,7 +68,7 @@
     col = lax.axis_index("col") * chans + lax.axis_index("chan")
     per = 128 // pw
     lgroups, rgroups = rd // per, cd // per
-    cuts = min(4, rgroups)
+    cuts = min(3, rgroups)
     depth = rn * sl
     steps = rd // cr
     cgroups = cr // per
@@ -85,7 +86,7 @@
         )
 
     loads = [pltpu.make_async_copy(far[n], near[n], w_sem.at[n]) for n in range(11)]
-    for n in (0, 1, 3, 4, 2, 6, 5, 7, 8, 9, 10):
+    for n in (1, 3, 4, 0, 2, 6, 5, 7, 8, 9, 10):
         loads[n].start()
     barrier = pltpu.get_barrier_semaphore()
 
@@ -102,7 +103,7 @@
         lax.broadcasted_iota(jnp.int32, (pw, 128), 1) % pw
         == lax.broadcasted_iota(jnp.int32, (pw, 128), 0)
     ).astype(F32).astype(BF16)
-    for n in (0, 1, 3, 4):
+    for n in (1, 3, 4):
         loads[n].wait()
     mask = mask_ref[...].astype(F32).astype(BF16)
     spots = tl // per
@@ -111,14 +112,18 @@
         == lax.broadcasted_iota(jnp.int32, (tl, spots * 128), 0)
     ).astype(F32).astype(BF16)
     wide_mask = dot(mask, token_of)
+    tiles = [
+        lax.dot_general(
+            w_ref[...], spread, (((0,), (0,)), ((), ())), preferred_element_type=F32
+        ).astype(BF16)
+        for w_ref in (wl_ref, wr_ref)
+    ]
+    loads[0].wait()
     feats = feat_ref[...].reshape(sl * tl, feat_ref.shape[2])
     lane_of = lax.broadcasted_iota(jnp.int32, (sl, 128), 1) // pw
 
-    def project(n, w_ref):
-        tiled = lax.dot_general(
-            w_ref[...], spread, (((0,), (0,)), ((), ())), preferred_element_type=F32
-        ).astype(BF16)
-        proj[n] = dot(feats, tiled)
+    def project(n):
+        proj[n] = dot(feats, tiles[n])
         parts = []
         for g in range(spots):
             got = proj[n, pl.ds(g * per, sl, stride=tl), :]
@@ -128,14 +133,14 @@
             parts.append((got * wide_mask[:, g * 128 : (g + 1) * 128]).astype(BF16))
         return parts
 
-    left = project(0, wl_ref)
+    left = project(0)
     for k in range(fold):
         for g in range(lgroups):
             lsend[k, 1 + g] = left[k * lgroups + g]
         lsend[k, 0] = jnp.zeros((sl, 128), BF16)
         lsend[k, 0, :, 0:rd] = mask[:, k * rd : (k + 1) * rd]
     def project_right():
-        right = project(1, wr_ref)
+        right = project(1)
         for g in range(rgroups):
             rg[row, 1 + g] = right[g]
         rg[row, 0] = jnp.zeros((sl, 128), BF16)
@@ -176,31 +181,35 @@
 
             @pl.when(jnp.logical_not(mine))
             def _():
-                remote(src, dst, l1_send.at[k, n], l1_recv.at[slot, n], to_row, to_col).start()
+                remote(src, dst, l1_send.at[k], l1_recv.at[slot, n], to_row, to_col).start()
 
     chips = cn // chans
 
     def spread_left(i, n, at_home):
         m = (row // chans + i) % held
+        first = isinstance(n, int) and n == 0
         piece = lg.at[m * chans + core, span(n)]
         pltpu.make_async_copy(piece, piece, l1_recv.at[m, n]).wait()
         if at_home:
             for d in range(1, chips):
+                there_chip = (chip + d) % chips * chans
                 remote(
-                    piece, piece, x_send.at[m, d - 1, n], l1_recv.at[m, n],
-                    row, (chip + d) % chips * chans + core,
+                    piece, piece, x_send.at[d - 1], l1_recv.at[m, n], row, there_chip + core
                 ).start()
-        for e in range(1, chans):
+                for e in range(1, chans if first else 0):
+                    remote(
+                        piece, piece, e_send.at[d - 1], l2_recv.at[n],
+                        row, there_chip + (core + e) % chans,
+                    ).start()
+        for e in range(1, chans if at_home or not first else 0):
             remote(
-                piece, piece, l2_send.at[m, e - 1, n], l2_recv.at[m, e - 1, n],
+                piece, piece, l2_send.at[0], l2_recv.at[n],
                 row, chip * chans + (core + e) % chans,
             ).start()
 
     def take_left(n):
-        for m in range(held):
-            for e in range(1, chans):
-                piece = lg.at[m * chans + (core + chans - e) % chans, span(n)]
-                pltpu.make_async_copy(piece, piece, l2_recv.at[m, e - 1, n]).wait()
+        got = lg.at[pl.ds(0, held * (chans - 1)), span(n)]
+        pltpu.make_async_copy(got, got, l2_recv.at[n]).wait()
 
     send_left(0)
 
@@ -214,10 +223,12 @@
         downs = jnp.logical_and(row + t < rn, row >= 1)
         return (ups, low, row + 1), (downs, high, row - 1)
 
-    quarter = rgroups // cuts
-    pieces = [
-        pl.ds(1 + e * quarter, quarter) if e else pl.ds(0, 1 + quarter) for e in range(cuts)
+    quarter = max(rgroups // 4, 1)
+    early_pieces = [
+        pl.ds(1 + e * quarter, quarter) if e else pl.ds(0, 1 + quarter)
+        for e in range(rgroups // 2 // quarter)
     ]
+    pieces = early_pieces + [pl.ds(1 + rgroups // 2, rgroups - rgroups // 2)]
 
     upward = chip < chips // 2
 
@@ -229,14 +240,15 @@
                 for e in cut_range(later):
                     part_of = rg.at[slot, pieces[e]]
                     remote(
-                        part_of, part_of, r_send.at[way, 0, e], r_recv.at[slot, e], to_row, col
+                        part_of, part_of, r_send.at[way, 0], r_recv.at[slot, e], to_row, col
                     ).start()
 
     def cut_range(later):
-        return range(cuts // 2, cuts) if later else range(cuts // 2)
+        return range(cuts - 1, cuts) if later else range(cuts - 1)
 
     pass_on(True, False)
     pass_on(False, False)
+    pass_on(True, True)
     for n in range(1, steps):
         send_left(n)
 
@@ -283,7 +295,7 @@
                 def _():
                     part_of = rg.at[slot, piece]
                     remote(
-                        part_of, part_of, r_send.at[way, t + 1, e], r_recv.at[slot, e],
+                        part_of, part_of, r_send.at[way, t + 1], r_recv.at[slot, e],
                         to_row, col,
                     ).start()
 
@@ -307,7 +319,7 @@
     def _():
         spread_left(0, 0, True)
 
-    @pl.when(jnp.logical_and(is_home, ends))
+    @pl.when(is_home)
     def _():
         for i in range(1, held):
             spread_left(i, 0, True)
@@ -318,17 +330,10 @@
             spread_left(i, 0, False)
 
     hops(0, 1, True)
-    pass_on(True, True)
-
     @pl.when(ends)
     def _():
         pass_on(False, True)
 
-
-    @pl.when(jnp.logical_and(is_home, inner))
-    def _():
-        for i in range(1, held):
-            spread_left(i, 0, True)
 
     hops(1, rn - 1, True)
 
@@ -352,6 +357,10 @@
     @pl.when(inner)
     def _():
         pass_on(False, True)
+
+    @pl.when(away)
+    def _():
+        hops(0, 1, True, True)
 
     take_left(0)
     left_mask = lg[:, 0].astype(F32).reshape(depth, 128)
@@ -380,6 +389,9 @@
 
     lag = 0
 
+    slots = 1 if chips == 2 else 2
+    final = steps - 1
+
     def segments(h):
         found = []
         for begin in range(h * half, (h + 1) * half, seg):
@@ -393,11 +405,13 @@
             across = to_col // chans != chip
             at_end = jnp.logical_or(to_row == 0, to_row == rn - 1)
             turned = jnp.logical_and(across, at_end)
+            if h == 1:
+                turned = jnp.logical_and(turned, step != final)
             sub = off // seg
             src = two.at[pl.ds(step * cr, cr), pl.ds(begin, seg)]
             dst = mirror.at[pl.ds(row % fold * rd + step * cr, cr), pl.ds(off, seg)]
             rsem = m_recv.at[row % fold, step, sub]
-            ssem = m_send.at[k, step, sub]
+            ssem = m_send.at[k]
 
             @pl.when(mine)
             def _():
@@ -405,7 +419,7 @@
 
             @pl.when(turned)
             def _():
-                slot = jnp.where(to_row == 0, 0, 1)
+                slot = jnp.where(to_row == 0, 0, slots - 1)
                 remote(
                     src, relay.at[slot, step, sub], ssem, rl_recv.at[slot, step, sub],
                     row, to_col,
@@ -415,14 +429,16 @@
             def _():
                 remote(src, dst, ssem, rsem, to_row, to_col).start()
 
-    def relayed(slot):
-        to_row = (0, rn - 1)[slot]
+    def relayed(way):
+        to_row = (0, rn - 1)[way]
         active = jnp.logical_and(col == row // fold, to_row // fold // chans != chip)
-        return active, to_row
+        return active, to_row, way % slots
 
     def forward(h, step):
-        for slot in range(2):
-            active, to_row = relayed(slot)
+        for way in range(2):
+            active, to_row, slot = relayed(way)
+            if h == 1:
+                active = jnp.logical_and(active, step != final)
             for _begin, k, off in segments(h):
                 if k == to_row % fold:
                     sub = off // seg
@@ -450,7 +466,7 @@
                         hop(t, way, True)
                     else:
 
-                        @pl.when(jnp.logical_or(away, upward == (way == 1)))
+                        @pl.when(upward == (way == 1))
                         def _():
                             hop(0, way, True)
 
@@ -466,11 +482,19 @@
     def one_step(h, step):
         lo = h * half
         if h == 0:
+
+            @pl.when(step > 0)
+            def _():
+                forward(h, step)
+
             serve(step)
 
-        @pl.when(step >= lag)
-        def _():
-            forward(h, step - lag)
+            @pl.when(step == 0)
+            def _():
+                forward(h, step)
+
+        else:
+            forward(h, step)
 
         if h and lag:
 
@@ -510,7 +534,8 @@
         normed = (shifted * lax.rsqrt(var + epsilon)).astype(BF16)
         gate = dot(normed, wg_ref[...])
         up = dot(normed, wu_ref[...])
-        hidden = (gate / (1.0 + jnp.exp(-gate)) * up).astype(BF16)
+        halved = gate * 0.5
+        hidden = ((halved + halved * jnp.tanh(halved)) * up).astype(BF16)
         done = (values + dot(hidden, wd_ref[...])).astype(BF16)
         two[pl.ds(step * cr, cr), lo : lo + half] = done.reshape(cr, half, ch)
         send_mirror(h, step)
@@ -568,36 +593,50 @@
 
         lax.fori_loop(top, top + seg, one_row, 0, unroll=4)
 
-    strip = min(32, rd)
+    top_rows = seg // 2 if subs > 1 else 0
+    blocks = [(0, top_rows)] if top_rows else []
+    while (blocks[-1][1] if blocks else 0) < rd:
+        first = blocks[-1][1] if blocks else 0
+        blocks.append((first, min(first + 32, rd)))
+
+    def conv_block(q, first, last):
+        begin = q * cr
+        count = last - first
+        total = sym[first:last, begin : begin + cr].reshape(count * cr, ch)
+        for a in range(3):
+            window = wide[first + a : last + a, begin : begin + cr]
+            total = total + dot(window.reshape(count * cr, 3 * ch), wk_ref[a])
+        total = total.reshape(count, cr, ch)
+        result[first:last, begin : begin + cr] = total.astype(BF16)
+        if q in (0, stripes - 1):
+            sym[first:last, begin : begin + cr] = total
+        else:
+            if first == 0:
+                sym[0, begin : begin + cr] = total[0]
+            if last == rd:
+                sym[rd - 1, begin : begin + cr] = total[count - 1]
 
     def conv(q):
-        begin = q * cr
-        for first in range(0, rd, strip):
-            total = sym[first : first + strip, begin : begin + cr].reshape(strip * cr, ch)
-            for a in range(3):
-                window = wide[first + a : first + a + strip, begin : begin + cr]
-                total = total + dot(window.reshape(strip * cr, 3 * ch), wk_ref[a])
-            total = total.reshape(strip, cr, ch)
-            result[first : first + strip, begin : begin + cr] = total.astype(BF16)
-            if q in (0, stripes - 1):
-                sym[first : first + strip, begin : begin + cr] = total
-            else:
-                if first == 0:
-                    sym[0, begin : begin + cr] = total[0]
-                if first + strip == rd:
-                    sym[rd - 1, begin : begin + cr] = total[strip - 1]
+        for first, last in blocks[1 if top_rows else 0 :]:
+            conv_block(q, first, last)
         if 0 < q < stripes - 1:
             middle(q).start()
 
     def middle(q):
         block = (pl.ds(1, rd - 2), pl.ds(q * cr, cr))
-        return pltpu.make_async_copy(result.at[block], out_ref.at[block], o_sem.at[0, q])
-
+        return pltpu.make_async_copy(result.at[block], out_ref.at[block], o_sem.at[0])
+
+    done = 0
     for sub in range(subs):
         for q in range(stripes):
             take_mirror(sub, q)
-            if sub == subs - 1 and 0 < q < stripes - 1:
+            if sub == 0 and top_rows and q:
+                conv_block(q - 1, 0, top_rows)
+            if sub == subs - 1 and 0 < q < stripes - 2:
                 conv(q - 1)
+                done = q
+        if sub == 0 and top_rows:
+            conv_block(stripes - 1, 0, top_rows)
 
     for n, (a, b) in enumerate(AROUND):
         if b == 0:
@@ -627,15 +666,19 @@
                 h_recv.at[n], row + a, col + b,
             ).start()
 
-    for q in range(max(stripes - 2, 0), stripes):
+    for q in range(done, stripes):
         conv(q)
 
-    for n, (a, b) in enumerate(AROUND):
-
-        @pl.when(there(-a, -b))
-        def _():
-            piece = hrecv.at[n, pl.ds(0, lines(a, b))]
-            pltpu.make_async_copy(piece, piece, h_recv.at[n]).wait()
+    def take_halo(wanted):
+        for n, (a, b) in enumerate(AROUND):
+            if wanted(a):
+
+                @pl.when(there(-a, -b))
+                def _():
+                    piece = hrecv.at[n, pl.ds(0, lines(a, b))]
+                    pltpu.make_async_copy(piece, piece, h_recv.at[n]).wait()
+
+    take_halo(lambda a: a == 0)
 
     slot_of = {direction: n for n, direction in enumerate(AROUND)}
     along = lax.broadcasted_iota(jnp.int32, (cd, ch), 0)
@@ -667,87 +710,86 @@
             + dot(below, wk_ref[2, lo : lo + ch])
         )
 
-    edge_row(1, 0)
-    edge_row(-1, rd - 1)
     colf[0] = edge_col(1)
     colf[1] = edge_col(-1)
-    for i in (0, rd - 1):
-        result[i] = sym[i].astype(BF16)
+    place16 = lax.broadcasted_iota(jnp.int32, (16, ch), 0)
 
     def patch_row(i, carry):
-        first = sym[i, 0:16]
+        first = sym[i, 0:16] + jnp.where(place16 == 0, colf[0, pl.ds(i, 1), :], 0.0)
         if cd == 16:
             first = first + jnp.where(place16 == 15, colf[1, pl.ds(i, 1), :], 0.0)
-        result[i, 0:16] = (
-            first + jnp.where(place16 == 0, colf[0, pl.ds(i, 1), :], 0.0)
-        ).astype(BF16)
+        result[i, 0:16] = first.astype(BF16)
         if cd > 16:
             result[i, cd - 16 : cd] = (
                 sym[i, cd - 16 : cd] + jnp.where(place16 == 15, colf[1, pl.ds(i, 1), :], 0.0)
             ).astype(BF16)
         return carry
 
-    place16 = lax.broadcasted_iota(jnp.int32, (16, ch), 0)
-    lax.fori_loop(0, rd, patch_row, 0, unroll=4)
-
-    closing = []
-    for n, i in enumerate((0, rd - 1)):
-        closing.append(pltpu.make_async_copy(result.at[i], out_ref.at[i], o_sem.at[1, n]))
+    lax.fori_loop(1, rd - 1, patch_row, 0, unroll=2)
+
     for n, q in enumerate((0, stripes - 1)):
         block = (pl.ds(1, rd - 2), pl.ds(q * cr, cr))
-        closing.append(
-            pltpu.make_async_copy(result.at[block], out_ref.at[block], o_sem.at[2, n])
-        )
-    for copy in closing:
-        copy.start()
+        pltpu.make_async_copy(result.at[block], out_ref.at[block], o_sem.at[2]).start()
+
+    take_halo(lambda a: a != 0)
+    for a, i in ((1, 0), (-1, rd - 1)):
+        edge_row(a, i)
+        total = sym[i]
+        total = total + jnp.where(along == 0, colf[0, i : i + 1, :], 0.0)
+        total = total + jnp.where(along == cd - 1, colf[1, i : i + 1, :], 0.0)
+        result[i] = total.astype(BF16)
+        pltpu.make_async_copy(result.at[i], out_ref.at[i], o_sem.at[1]).start()
 
     for k in range(fold):
         @pl.when(jnp.logical_not(l1_target(k)[2]))
         def _():
-            for n in range(steps):
-                piece = lsend.at[k, span(n)]
-                pltpu.make_async_copy(piece, piece, l1_send.at[k, n]).wait()
+            pltpu.make_async_copy(lsend.at[k], lsend.at[k], l1_send.at[k]).wait()
 
         to_row, to_col = col * fold + k, row // fold
 
         @pl.when(jnp.logical_not(jnp.logical_and(to_row == row, to_col == col)))
         def _():
-            for step in range(steps):
-                for sub in range(subs):
-                    src = two.at[pl.ds(step * cr, cr), pl.ds(k * rd + sub * seg, seg)]
-                    pltpu.make_async_copy(src, src, m_send.at[k, step, sub]).wait()
-
-    for slot in range(2):
-
-        @pl.when(relayed(slot)[0])
-        def _():
-            for step in range(steps):
-                for sub in range(subs):
-                    piece = relay.at[slot, step, sub]
-                    pltpu.make_async_copy(piece, piece, rl_send.at[slot, step, sub]).wait()
+            src = two.at[pl.ds(0, rd), pl.ds(k * rd, rd)]
+            pltpu.make_async_copy(src, src, m_send.at[k]).wait()
+
+    for way in range(2):
+        active, to_row, slot = relayed(way)
+        for h in range(2):
+            for _begin, k, off in segments(h):
+                count = steps - 1 if h == 1 else steps
+                if k == to_row % fold and count:
+
+                    @pl.when(active)
+                    def _():
+                        for step in range(count):
+                            piece = relay.at[slot, step, off // seg]
+                            pltpu.make_async_copy(
+                                piece, piece, rl_send.at[slot, step, off // seg]
+                            ).wait()
 
     for t in range(rn - 1):
         for way, (go, slot, _to_row) in enumerate(chain(t)):
 
             @pl.when(go)
             def _():
-                for e, piece in enumerate(pieces):
-                    part_of = rg.at[slot, piece]
-                    pltpu.make_async_copy(part_of, part_of, r_send.at[way, t, e]).wait()
-
-    for m in range(held):
-        for n in range(steps):
-            piece = lg.at[m * chans + core, span(n)]
-            for e in range(1, chans):
-                pltpu.make_async_copy(piece, piece, l2_send.at[m, e - 1, n]).wait()
+                pltpu.make_async_copy(rg.at[slot], rg.at[slot], r_send.at[way, t]).wait()
+
+    others = pl.ds(0, held * (chans - 1))
+    if steps > 1:
+
+        @pl.when(away)
+        def _():
+            got = lg.at[others, pl.ds(1 + cgroups, (steps - 1) * cgroups)]
+            pltpu.make_async_copy(got, got, l2_send.at[0]).wait()
 
     @pl.when(is_home)
     def _():
-        for m in range(held):
-            for n in range(steps):
-                piece = lg.at[m * chans + core, span(n)]
-                for d in range(1, chips):
-                    pltpu.make_async_copy(piece, piece, x_send.at[m, d - 1, n]).wait()
+        pltpu.make_async_copy(lg.at[others], lg.at[others], l2_send.at[0]).wait()
+        for d in range(1, chips):
+            got = lg.at[pl.ds(0, held)]
+            pltpu.make_async_copy(got, got, x_send.at[d - 1]).wait()
+            got = lg.at[others, span(0)]
+            pltpu.make_async_copy(got, got, e_send.at[d - 1]).wait()
 
     for n, (a, b) in enumerate(AROUND):
 
@@ -755,10 +797,13 @@
         def _():
             piece = hsend.at[n, pl.ds(0, lines(a, b))]
             pltpu.make_async_copy(piece, piece, h_send.at[n]).wait()
-    for q in range(1, stripes - 1):
-        middle(q).wait()
-    for copy in closing:
-        copy.wait()
+    if stripes > 2:
+        block = (pl.ds(1, rd - 2), pl.ds(cr, cd - 2 * cr))
+        pltpu.make_async_copy(result.at[block], out_ref.at[block], o_sem.at[0]).wait()
+    block = pl.ds(0, 2)
+    pltpu.make_async_copy(result.at[block], out_ref.at[block], o_sem.at[1]).wait()
+    block = (pl.ds(1, rd - 2), pl.ds(0, 2 * cr))
+    pltpu.make_async_copy(result.at[block], out_ref.at[block], o_sem.at[2]).wait()
 
 
 def on_device(
@@ -791,8 +836,9 @@
     seg = min(half, rd)
     subs = rd // seg
     groups, rgroups = rd // per, cd // per
-    cuts = min(4, rgroups)
+    cuts = min(3, rgroups)
     held = rn // chans
+    slots = 1 if cn // chans == 2 else 2
     sizes = (rn, cn, chans, fold, rd, cd, ch, sl, tl, pw, cr)
     operands = (
         alignment_features,
@@ -840,21 +886,22 @@
             pltpu.VMEM((8, tall, ch), BF16),
             pltpu.VMEM((8, tall, ch), BF16),
             pltpu.VMEM((rd, cd, ch), BF16),
-            dma((fold, steps)),
+            dma((fold,)),
             dma((held, steps)),
-            dma((held, max(cn // chans - 1, 1), steps)),
-            dma((held, max(chans - 1, 1), steps)),
-            dma((held, max(chans - 1, 1), steps)),
-            dma((2, rn - 1, cuts)),
+            dma((max(cn // chans - 1, 1),)),
+            dma((max(cn // chans - 1, 1),)),
+            dma((1,)),
+            dma((steps,)),
+            dma((2, rn - 1)),
             dma((rn, cuts)),
+            dma((fold,)),
             dma((fold, steps, subs)),
-            dma((fold, steps, subs)),
-            pltpu.VMEM((2, steps, subs, cr, seg, ch), BF16),
-            dma((2, steps, subs)),
-            dma((2, steps, subs)),
+            pltpu.VMEM((slots, steps, subs, cr, seg, ch), BF16),
+            dma((slots, steps, subs)),
+            dma((slots, steps, subs)),
             dma((8,)),
             dma((8,)),
-            dma((3, max(cd // cr, 2))),
+            dma((3,)),
         ],
         compiler_params=pltpu.CompilerParams(
             collective_id=0, has_side_effects=True, vmem_limit_bytes=44 * 1024 * 1024

time: 52.8 us -> 51.4 us (0.973)
  Pallas kernels: 51.7 us -> 50.2 us
    pallas_call x1, Pallas kernels: 51.7 us -> 50.2 us  [on_device(): pl.pallas_call(functools.partial(block_kernel, sizes), out_shape=jax.Shap...]
where the time goes in v3:
time: 51.4 us; the launch traced here: 51.2 us
  Pallas kernels  50.2 us (98%)
  local copies, waits for them, and re-layouts  0.97 us (2%)
    pallas_call x1, Pallas kernels, on_device(): pl.pallas_call(functools.partial(block_kernel, sizes), out_shape=jax.Shap...  50.2 us

profile of v3, /device:TPU:1, one launch (start us, length us, event | category | flops | bytes accessed | tf_op | source)
XLA Modules:
  0.0 51.2 jit_solution(11946341571049759098)
XLA Ops:
  0.0 50.2 %shard_map.109 = bf16[64,64,128]{2,1,0:T(8,128)(2,1)S(1)} custom-call(bf16[32,64,64]{2,1,0:T(8,128)(2,1)} %refs_0_.1, s32[32,64]{1,0:T(8,128)} %refs_1_.1, s32[1,256]{1,0:T(1,128)} %bitcast.7, bf16[32,64]{1,0:T(8,128)(2,1)} %bitcast.5, bf16[32,64]{1,0:T(8,128)(2,1)} %bitcast.6, bf16[64,64,128]{2,1,0:T(8,128)(2,1)} %refs_5_.1, bf16[1024,128]{1,0:T(8,128)(2,1)} %refs_6_.1, ...), custom_call_target="tpu_custom_call" | custom-call | tf_op jit(solution)/shard_map/pallas_call | solution.py:858
  50.2 1.0 %copy.13 = bf16[64,64,128]{2,1,0:T(8,128)(2,1)} copy(bf16[64,64,128]{2,1,0:T(8,128)(2,1)S(1)} %shard_map.109) | data formatting | bytes 2097152

commit v4 on v3

--- a/solution.py
+++ b/solution.py
@@ -57,6 +57,9 @@
     m_send,
     m_recv,
     relay,
+    extra,
+    ex_send,
+    ex_recv,
     rl_send,
     rl_recv,
     h_send,
@@ -335,6 +338,8 @@
         pass_on(False, True)
 
 
+    hops(0, 1, False)
+
     hops(1, rn - 1, True)
 
     @pl.when(jnp.logical_and(away, inner))
@@ -352,7 +357,7 @@
     def _():
         hops(0, 1, True, True)
 
-    hops(0, rn - 1, False)
+    hops(1, rn - 1, False)
 
     @pl.when(inner)
     def _():
@@ -399,7 +404,7 @@
         return found
 
     def send_mirror(h, step):
-        for begin, k, off in segments(h):
+        for g, (begin, k, off) in enumerate(segments(h)):
             to_row, to_col = col * fold + k, row // fold
             mine = jnp.logical_and(to_row == row, to_col == col)
             across = to_col // chans != chip
@@ -407,6 +412,9 @@
             turned = jnp.logical_and(across, at_end)
             if h == 1:
                 turned = jnp.logical_and(turned, step != final)
+            bent = jnp.logical_and(across, jnp.logical_not(at_end))
+            bent = bent & inner & jnp.logical_not(upward)
+            bent = jnp.logical_and(bent, step == 0) if h == 1 else False
             sub = off // seg
             src = two.at[pl.ds(step * cr, cr), pl.ds(begin, seg)]
             dst = mirror.at[pl.ds(row % fold * rd + step * cr, cr), pl.ds(off, seg)]
@@ -425,7 +433,16 @@
                     row, to_col,
                 ).start()
 
-            @pl.when(jnp.logical_not(jnp.logical_or(mine, turned)))
+            if h == 1:
+
+                @pl.when(bent)
+                def _():
+                    slot = (col + 2 * cn - (to_col // chans + 1) * chans) % cn
+                    remote(
+                        src, extra.at[slot, g], ssem, ex_recv.at[slot, g], row, to_col
+                    ).start()
+
+            @pl.when(jnp.logical_not(mine | turned | bent))
             def _():
                 remote(src, dst, ssem, rsem, to_row, to_col).start()
 
@@ -454,12 +471,43 @@
                             m_recv.at[row % fold, step, sub], to_row, col,
                         ).start()
 
+    def bend():
+        for slot in range(cn - chans):
+            from_col = ((chip + 1) * chans + slot) % cn
+            for g, (_begin, k, off) in enumerate(segments(1)):
+                to_row = from_col * fold + k
+                active = (col == row // fold) & inner & (to_row != 0) & (to_row != rn - 1)
+                active = active & (from_col // chans >= chips // 2)
+
+                @pl.when(active)
+                def _():
+                    piece = extra.at[slot, g]
+                    pltpu.make_async_copy(piece, piece, ex_recv.at[slot, g]).wait()
+                    remote(
+                        piece, mirror.at[pl.ds(row % fold * rd, cr), pl.ds(off, seg)],
+                        ex_send.at[slot, g], m_recv.at[row % fold, 0, off // seg],
+                        to_row, col,
+                    ).start()
+
+    def unbend():
+        for slot in range(cn - chans):
+            from_col = ((chip + 1) * chans + slot) % cn
+            for g, (_begin, k, _off) in enumerate(segments(1)):
+                to_row = from_col * fold + k
+                active = (col == row // fold) & inner & (to_row != 0) & (to_row != rn - 1)
+                active = active & (from_col // chans >= chips // 2)
+
+                @pl.when(active)
+                def _():
+                    piece = extra.at[slot, g]
+                    pltpu.make_async_copy(piece, piece, ex_send.at[slot, g]).wait()
+
     low_lanes = lax.broadcasted_iota(jnp.int32, (depth, 128), 1) < 64
 
     def serve(step):
         for t in range(rn - 1):
 
-            @pl.when(step == min(t, steps - 1))
+            @pl.when(step == jnp.where(ends, steps - 1, min(t, steps - 1)))
             def _():
                 for way in (0, 1):
                     if t:
@@ -483,18 +531,26 @@
         lo = h * half
         if h == 0:
 
-            @pl.when(step > 0)
+            @pl.when(inner & (step > 0))
             def _():
                 forward(h, step)
 
             serve(step)
 
-            @pl.when(step == 0)
+            @pl.when(inner & (step == 0))
             def _():
                 forward(h, step)
 
         else:
-            forward(h, step)
+
+            @pl.when(inner)
+            def _():
+                forward(h, step)
+
+            @pl.when(step == min(2, steps - 1))
+            def _():
+                bend()
+
 
         if h and lag:
 
@@ -540,6 +596,11 @@
         two[pl.ds(step * cr, cr), lo : lo + half] = done.reshape(cr, half, ch)
         send_mirror(h, step)
 
+        @pl.when(ends)
+        def _():
+            forward(h, step)
+
+
     def run(h):
         def body(step, carry):
             one_step(h, step)
@@ -626,45 +687,53 @@
         block = (pl.ds(1, rd - 2), pl.ds(q * cr, cr))
         return pltpu.make_async_copy(result.at[block], out_ref.at[block], o_sem.at[0])
 
+    def there(a, b):
+        r, c = row + a, col + b
+        return jnp.logical_and(
+            jnp.logical_and(r >= 0, r < rn), jnp.logical_and(c >= 0, c < cn)
+        )
+
+    def lines(a, b):
+        return cd if b == 0 else (rd if a == 0 else 16)
+
+    def send_halo(ready):
+        for n, (a, b) in enumerate(AROUND):
+            if not ready(a, b):
+                continue
+            size = lines(a, b)
+            side = 0 if b < 0 else 1
+            if b == 0:
+                hsend[n, 0:cd] = wide[1 if a < 0 else rd, :, ch : 2 * ch]
+            elif a == 0:
+                hsend[n, 0:rd] = colf[side].astype(BF16)
+            else:
+                corner = colf[side, 0:1] if a < 0 else colf[side, rd - 1 : rd]
+                hsend[n, 0:16] = jnp.broadcast_to(corner, (16, ch)).astype(BF16)
+
+            @pl.when(there(a, b))
+            def _():
+                remote(
+                    hsend.at[n, pl.ds(0, size)], hrecv.at[n, pl.ds(0, size)], h_send.at[n],
+                    h_recv.at[n], row + a, col + b,
+                ).start()
+
     done = 0
     for sub in range(subs):
         for q in range(stripes):
             take_mirror(sub, q)
+            if sub == subs - 1 and q == 0:
+                send_halo(lambda a, b: b < 0 and a >= 0)
             if sub == 0 and top_rows and q:
                 conv_block(q - 1, 0, top_rows)
             if sub == subs - 1 and 0 < q < stripes - 2:
                 conv(q - 1)
                 done = q
+        if sub == 0 and subs > 1:
+            send_halo(lambda a, b: a < 0)
         if sub == 0 and top_rows:
             conv_block(stripes - 1, 0, top_rows)
 
-    for n, (a, b) in enumerate(AROUND):
-        if b == 0:
-            hsend[n, 0:cd] = wide[1 if a < 0 else rd, :, ch : 2 * ch]
-        elif a == 0:
-            hsend[n, 0:rd] = colf[0 if b < 0 else 1].astype(BF16)
-        else:
-            corner = colf[0 if b < 0 else 1, 0:1] if a < 0 else colf[0 if b < 0 else 1, rd - 1 : rd]
-            hsend[n, 0:16] = jnp.broadcast_to(corner, (16, ch)).astype(BF16)
-
-    def there(a, b):
-        r, c = row + a, col + b
-        return jnp.logical_and(
-            jnp.logical_and(r >= 0, r < rn), jnp.logical_and(c >= 0, c < cn)
-        )
-
-    def lines(a, b):
-        return cd if b == 0 else (rd if a == 0 else 16)
-
-    for n, (a, b) in enumerate(AROUND):
-
-        @pl.when(there(a, b))
-        def _():
-            size = lines(a, b)
-            remote(
-                hsend.at[n, pl.ds(0, size)], hrecv.at[n, pl.ds(0, size)], h_send.at[n],
-                h_recv.at[n], row + a, col + b,
-            ).start()
+    send_halo(lambda a, b: not (a < 0 and subs > 1) and not (b < 0 and a >= 0))
 
     for q in range(done, stripes):
         conv(q)
@@ -752,6 +821,7 @@
             src = two.at[pl.ds(0, rd), pl.ds(k * rd, rd)]
             pltpu.make_async_copy(src, src, m_send.at[k]).wait()
 
+    unbend()
     for way in range(2):
         active, to_row, slot = relayed(way)
         for h in range(2):
@@ -897,6 +967,9 @@
             dma((fold,)),
             dma((fold, steps, subs)),
             pltpu.VMEM((slots, steps, subs, cr, seg, ch), BF16),
+            pltpu.VMEM((max(cn - chans, 1), half // seg, cr, seg, ch), BF16),
+            dma((max(cn - chans, 1), half // seg)),
+            dma((max(cn - chans, 1), half // seg)),
             dma((slots, steps, subs)),
             dma((slots, steps, subs)),
             dma((8,)),

time: 51.4 us -> 50.4 us (0.981)
  the two profiles are of different devices: /device:TPU:1 before, /device:TPU:17 now
where the time goes in v4:
time: 50.4 us; the launch traced here: 50.2 us
  Pallas kernels  49.2 us (98%)
  local copies, waits for them, and re-layouts  0.97 us (2%)
    pallas_call x1, Pallas kernels, on_device(): pl.pallas_call(functools.partial(block_kernel, sizes), out_shape=jax.Shap...  49.2 us

profile of v4, /device:TPU:17, one launch (start us, length us, event | category | flops | bytes accessed | tf_op | source)
XLA Modules:
  0.0 50.2 jit_solution(4136710152500665585)
XLA Ops:
  0.0 49.2 %shard_map.109 = bf16[64,64,128]{2,1,0:T(8,128)(2,1)S(1)} custom-call(bf16[32,64,64]{2,1,0:T(8,128)(2,1)} %refs_0_.1, s32[32,64]{1,0:T(8,128)} %refs_1_.1, s32[1,256]{1,0:T(1,128)} %bitcast.7, bf16[32,64]{1,0:T(8,128)(2,1)} %bitcast.5, bf16[32,64]{1,0:T(8,128)(2,1)} %bitcast.6, bf16[64,64,128]{2,1,0:T(8,128)(2,1)} %refs_5_.1, bf16[1024,128]{1,0:T(8,128)(2,1)} %refs_6_.1, ...), custom_call_target="tpu_custom_call" | custom-call | tf_op jit(solution)/shard_map/pallas_call | solution.py:928
  49.3 1.0 %copy.13 = bf16[64,64,128]{2,1,0:T(8,128)(2,1)} copy(bf16[64,64,128]{2,1,0:T(8,128)(2,1)S(1)} %shard_map.109) | data formatting | bytes 2097152

commit v5 on v4

--- a/solution.py
+++ b/solution.py
@@ -652,7 +652,7 @@
             colf[1, pl.ds(i, 1), :] = masked[cr - 1 : cr]
             return carry
 
-        lax.fori_loop(top, top + seg, one_row, 0, unroll=4)
+        lax.fori_loop(top, top + seg, one_row, 0, unroll=8)
 
     top_rows = seg // 2 if subs > 1 else 0
     blocks = [(0, top_rows)] if top_rows else []

time: 50.4 us -> 50.3 us (level)
  no operation moved by 1% of the time
where the time goes in v5:
time: 50.3 us; the launch traced here: 50.1 us
  Pallas kernels  49.1 us (98%)
  local copies, waits for them, and re-layouts  0.97 us (2%)
    pallas_call x1, Pallas kernels, on_device(): pl.pallas_call(functools.partial(block_kernel, sizes), out_shape=jax.Shap...  49.1 us

profile of v5, /device:TPU:17, one launch (start us, length us, event | category | flops | bytes accessed | tf_op | source)
XLA Modules:
  0.0 50.1 jit_solution(2105948373726709666)
XLA Ops:
  0.0 49.1 %shard_map.109 = bf16[64,64,128]{2,1,0:T(8,128)(2,1)S(1)} custom-call(bf16[32,64,64]{2,1,0:T(8,128)(2,1)} %refs_0_.1, s32[32,64]{1,0:T(8,128)} %refs_1_.1, s32[1,256]{1,0:T(1,128)} %bitcast.7, bf16[32,64]{1,0:T(8,128)(2,1)} %bitcast.5, bf16[32,64]{1,0:T(8,128)(2,1)} %bitcast.6, bf16[64,64,128]{2,1,0:T(8,128)(2,1)} %refs_5_.1, bf16[1024,128]{1,0:T(8,128)(2,1)} %refs_6_.1, ...), custom_call_target="tpu_custom_call" | custom-call | tf_op jit(solution)/shard_map/pallas_call | solution.py:928
  49.1 1.0 %copy.13 = bf16[64,64,128]{2,1,0:T(8,128)(2,1)} copy(bf16[64,64,128]{2,1,0:T(8,128)(2,1)S(1)} %shard_map.109) | data formatting | bytes 2097152
